TPU v7x, 32 devices: a whole 2x2x4 slice. The times are simulated.
32 devices in a mesh: row: 8 (over y, x, core), col: 4 (over z).
Axes of the slice: x: 2, y: 2, z: 4, core: 2. Of those that a mesh axis runs over, the one named last changes fastest.
Arguments:
- row_vectors: float32 [2048, 512], P('row', 'col'), may hold values from -0.05 to 0.05
- column_vectors: float32 [3072, 512], P(('col', 'row')), may hold values from -0.05 to 0.05
- occupation: float32 [512], replicated, may hold values from 0.1 to 4
- phi_row: float32 [32, 256, 256], P(('row', 'col')), may hold values from -6 to 6
- phi_col: float32 [32, 256, 1024], P(('row', 'col')), may hold values from -6 to 6
- potential: float32 [32, 256], P(('row', 'col')), may hold values from -6 to 6
- tile_owner: int32 [32, 8], P('row'), may hold values from 0 to 3, as said below
- tile_slot: int32 [32, 8], P('row'), may hold values from 0 to 5, as said below
- correlation: int32 [32, 8], P('row'), may hold values 0 or 1
Outputs:
- density: float32 [32, 256], P(('row', 'col'))
- potential_rows: float32 [32, 256], P(('row', 'col'))
Inputs may be any that keep to these rules, and one draw needn't show every extreme that they name: `tile_owner`: within a row, at most two entries name the same holder, and in every row some holder is named by two entries. `tile_slot`: entries of one row with the same holder name different positions, so a batch's tiles are distinct.
All inputs are finite; a program needn't handle non-finite values. No bound on the sum of `correlation` on one device may be relied on, other than what follows from the above.
Results may differ from a plain program's by a relative error of at most 0.0003.
Values sent between devices are 32-bit elements; how exact they have to be, the bound alone decides.
No kernel may reach another device: no remote copies, remote signals or barrier semaphores. Data moves between devices by JAX's collectives and lax.ppermute only.
A program may use at most 64 MiB of HBM per device.

v0:
```python
import jax
import jax.numpy as jnp
from jax import lax
from jax.sharding import PartitionSpec as P

TW = 128
TPD = 6
TB = 8


def per_device(
    row_vectors,
    column_vectors,
    occupation,
    phi_row,
    phi_col,
    potential,
    tile_owner,
    tile_slot,
    correlation,
):
    states = lax.all_gather(row_vectors, "col", axis=1, tiled=True)
    scaled = states * occupation[None, :]
    density_block = lax.dot_general(
        scaled,
        lax.all_gather(column_vectors, "row", axis=0, tiled=True),
        (((1,), (1,)), ((), ())),
        precision=lax.Precision.HIGHEST,
        preferred_element_type=jnp.float32,
    )
    row_count = density_block.shape[0]
    groups = lax.axis_size("col")
    column = lax.axis_index("col")
    owners = tile_owner[column]
    slots = tile_slot[column]
    weights = correlation[column].astype(jnp.float32)
    strip_row = lax.all_gather(density_block, "col", axis=1, tiled=True)
    all_tiles = strip_row.reshape(row_count, groups * TPD, TW)
    strips = jnp.take(all_tiles, owners * TPD + slots, axis=1) * weights[None, :, None]
    points = phi_col.shape[1]
    columns_field = phi_col[0].reshape(points, TB, TW)
    coupled = jnp.einsum(
        "mkn,pkn->pm",
        strips,
        columns_field,
        precision=lax.Precision.HIGHEST,
        preferred_element_type=jnp.float32,
    )
    rows_field = phi_row[0]
    density = jnp.sum(rows_field * coupled, axis=1)
    potential_rows = jnp.sum(potential[0][:, None] * rows_field * coupled, axis=0)
    return (density[None, :], potential_rows[None, :])


def solution(mesh):
    in_specs = (
        P("row", "col"),
        P(("col", "row"), None),
        P(),
        P(("row", "col"), None, None),
        P(("row", "col"), None, None),
        P(("row", "col"), None),
        P("row", None),
        P("row", None),
        P("row", None),
    )
    out_specs = (P(("row", "col"), None), P(("row", "col"), None))
    return jax.shard_map(
        per_device, mesh=mesh, in_specs=in_specs, out_specs=out_specs, check_vma=False
    )
```

profile of v0, /device:TPU:0, one launch (start us, length us, event | category | flops | bytes accessed | tf_op | source)
XLA Modules:
  0.0 119.6 jit_solution(12351370189158188801)
XLA Ops:
  7.2 0.0 copy-start
  7.2 0.0 all-gather.3.cloned.1.call-start
  7.2 0.7 all-gather.3.cloned.1.call-update
  7.9 0.0 copy-start.1
  7.9 0.0 all-gather.5.cloned.1.call-start
  8.0 17.7 %all_gather.9 = f32[256,512]{1,0:T(8,128)S(1)} all-gather(f32[256,128]{1,0:T(8,128)} %param.9), channel_id=1, replica_groups=mesh['row'=8,'col'=4] {'col'}, dimensions={1}, use_global_device_ids=true | all-gather | bytes 655360 | tf_op jit(solution)/shard_map/all_gather | solution.py:22
  25.7 12.5 %all-gather.3.cloned.1.call-done = f32[768,512]{1,0:T(8,128)} async-done(((f32[96,512]{1,0:T(8,128)}), f32[768,512]{1,0:T(8,128)}) %all-gather.3.cloned.1.call-update) | async-done | bytes 1572880 | tf_op jit(solution)/shard_map/all_gather | solution.py:26
  38.2 3.8 %fusion.6 = f32[256,768]{1,0:T(8,128)} fusion(f32[768,512]{1,0:T(8,128)} %all-gather.3.cloned.1.call-done, f32[256,512]{1,0:T(8,128)S(1)} %all_gather.9, f32[512]{0:T(512)} %param.11), kind=kOutput, calls=%fused_computation.9 | convolution fusion | flops 1208090624 | bytes 2885632 | tf_op jit(solution)/shard_map/dot_general | solution.py:24
  42.0 0.0 all-gather.5.cloned.1.call-update
  42.0 0.0 copy-done
  42.0 1.2 copy.17
  43.2 0.0 copy-done.1
  43.2 0.1 copy.13
  43.3 0.7 fusion.16
  44.0 0.7 compare_and_fusion
  44.8 0.0 copy-start.2
  44.8 60.8 %all-gather.5.cloned.1.call-done = f32[256,3072]{1,0:T(8,128)} async-done(((f32[256,768]{1,0:T(8,128)}), f32[256,3072]{1,0:T(8,128)}) %all-gather.5.cloned.1.call-update) | async-done | bytes 3145744 | tf_op jit(solution)/shard_map/all_gather | solution.py:37
  105.6 2.2 %copy_bitcast_fusion = f32[256,24,128]{2,0,1:T(8,128)S(1)} fusion(f32[256,3072]{1,0:T(8,128)} %all-gather.5.cloned.1.call-done), kind=kLoop, calls=%fused_computation.1 | loop fusion | bytes 6291456 | tf_op jit(solution)/shard_map/reshape | solution.py:38
  107.9 1.6 %gather_fusion = f32[8,256,128]{2,1,0:T(8,128)} fusion(f32[256,24,128]{2,0,1:T(8,128)S(1)} %copy_bitcast_fusion, s32[1024]{0:T(1024)S(1)} %pad_clamp_fusion), kind=kCustom, calls=%fused_computation | custom fusion | bytes 2097184 | tf_op jit(solution)/shard_map/jit(_take)/gather | solution.py:39
  109.4 0.0 copy-done.2
  109.4 3.3 %fusion.11 = (f32[256]{0:T(256)}, f32[256]{0:T(256)}) fusion(f32[1,256,256]{1,2,0:T(8,128)S(1)} %copy.13, f32[256]{0:T(256)S(1)} %bitcast.40, f32[256,8,128]{2,1,0:T(8,128)} %bitcast.38, f32[8,256,128]{2,1,0:T(8,128)} %gather_fusion, f32[8]{0:T(128)S(1)} %fusion.16, pred[8]{0:T(512)(128)(4,1)S(1)} %get-tuple-element.4), kind=kOutput, calls=%fused_computation.16 | convolution fusion | flops 806157824 | bytes 2362408 | tf_op jit(solution)/shard_map/mkn,pkn->pm/dot_general | solution.py:42
  (2 shorter events, 0.0 us)
Async XLA Ops:
  7.2 34.9 %copy-start = (f32[1,256,1024]{2,1,0:T(8,128)S(1)}, f32[1,256,1024]{2,1,0:T(8,128)}, u32[]{:S(2)}) copy-start(f32[1,256,1024]{2,1,0:T(8,128)} %param.13) | copy-start | bytes 3145732
  7.2 31.0 %all-gather.3.cloned.1.call-start = ((), (), s32[]{:S(2)}) async-start(), calls=%async_computation | async-start | bytes 1769472 | tf_op jit(solution)/shard_map/all_gather | solution.py:26
  7.9 35.3 %copy-start.1 = (f32[1,256,256]{2,1,0:T(8,128)S(1)}, f32[1,256,256]{2,1,0:T(8,128)}, u32[]{:S(2)}) copy-start(f32[1,256,256]{2,1,0:T(8,128)} %param.12) | copy-start | bytes 786436
  7.9 97.7 %all-gather.5.cloned.1.call-start = ((), (), s32[]{:S(2)}) async-start(), calls=%async_computation.1 | async-start | bytes 3932160 | tf_op jit(solution)/shard_map/all_gather | solution.py:37
  44.8 64.7 %copy-start.2 = (f32[1,256]{1,0:T(1,128)S(1)}, f32[1,256]{1,0:T(1,128)}, u32[]{:S(2)}) copy-start(f32[1,256]{1,0:T(1,128)} %param.14) | copy-start | bytes 3076
Sparse Core Ops, SparseCore 0:
  9.9 28.2 all-gather.2
  42.1 63.4 all-gather.4
where the time goes:
time: 120 us
  waiting for transfers between devices  74 us (62%)
  blocking collectives  17.7 us (15%)
  between operations  14.1 us (12%)
  matrix products  7.11 us (6%)
  local copies, waits for them, and re-layouts  5.14 us (4%)
  other arithmetic  1.41 us (1%)
    all_gather x1, waiting for transfers between devices, per_device(): strip_row = lax.all_gather(density_block, 'col', axis=1, tiled=True)  60.8 us
    all_gather x1, blocking collectives, per_device(): states = lax.all_gather(row_vectors, 'col', axis=1, tiled=True)  17.7 us
    all_gather x1, waiting for transfers between devices, per_device(): lax.all_gather(column_vectors, 'row', axis=0, tiled=True)  12.5 us
    dot_general x1, matrix products, per_device(): lax.dot_general(scaled, lax.all_gather(column_vectors, 'row', axis=0, til...  3.8 us
    dot_general x1, matrix products, per_device(): jnp.einsum('mkn,pkn->pm', strips, columns_field, precision=lax.Precision....  3.31 us
  transfers between devices with their start and end apart: 2, of which 2 were waited for; matrix products, arithmetic and copies ran while one was open for 2% of the time, Pallas kernels for 0%

commit v1 on v0

v1 whole, which is shorter than its diff:
```python
import functools

import jax
import jax.numpy as jnp
from jax import lax
from jax.experimental import pallas as pl
from jax.experimental.pallas import tpu as pltpu
from jax.sharding import PartitionSpec as P


TW = 128
PAIR = 2
NT = (((1,), (1,)), ((), ()))
PARAMS = pltpu.CompilerParams(vmem_limit_bytes=16 << 20)
VMEM = pl.BlockSpec(memory_space=pltpu.VMEM)
HBM = pl.BlockSpec(memory_space=pltpu.HBM)
SMEM = pl.BlockSpec(memory_space=pltpu.SMEM)


def split(x):
    high = x.astype(jnp.bfloat16)
    return high, (x - high.astype(jnp.float32)).astype(jnp.bfloat16)


def dot3(a, b):
    (ah, al), (bh, bl) = a, b
    one = functools.partial(
        lax.dot_general, dimension_numbers=NT, preferred_element_type=jnp.float32
    )
    return one(ah, bh) + (one(ah, bl) + one(al, bh))


def flip(x, axis, bit):
    size = lax.axis_size(axis)
    return lax.ppermute(x, axis, [(i, i ^ bit) for i in range(size)])


def gather_rows(x):
    pieces = {0: x}
    bit = lax.axis_size("col") // 2
    while bit:
        for k, v in list(pieces.items()):
            pieces[k ^ bit] = flip(v, "col", bit)
        bit //= 2
    return [pieces[k] for k in range(len(pieces))]


def gather_columns(x):
    if lax.axis_size("row") != 8:
        return [lax.all_gather(x, "row", axis=0, tiled=True)]
    pieces = {0: x}
    for far in (2, 4, 6):
        pieces[far] = flip(x, "row", far)
    for near in (0, 2, 4, 6):
        pieces[near ^ 1] = flip(pieces[near], "row", 1)
    return [pieces[k] for k in range(8)]


def place(row, pieces, k):
    size = pieces[k].shape[0]
    if len(pieces) == 1:
        return pl.ds(0, size)
    return pl.ds(pl.multiple_of((row ^ k) * size, 32), size)


def requests(owner_ref, values_ref, batch, holder):
    found = [jnp.int32(0)] * PAIR
    count = jnp.int32(0)
    for t in range(owner_ref.shape[1]):
        hit = owner_ref[batch, t] == holder
        value = values_ref[batch, t] if values_ref is not None else jnp.int32(t)
        for k in range(PAIR):
            found[k] = jnp.where(hit & (count == k), value, found[k])
        count = count + hit.astype(jnp.int32)
    return found, count


def tile(ref, slot):
    return ref[pl.ds(pl.multiple_of(slot * TW, TW), TW), :]


def prepare_kernel(served, far, *refs):
    sources, refs = refs[:8], refs[8:]
    slots_out, row_out, hi_out, lo_out, occ_ref, phi_hi, phi_lo, pot_out = refs[:8]
    owner_ref, slot_ref, corr_ref, row_ref, chunk_ref, phi_ref, pot_ref, sems = refs[8:]
    targets = owner_ref, slot_ref, corr_ref, row_ref, chunk_ref, occ_ref, phi_ref, pot_ref
    copies = [
        pltpu.make_async_copy(source, target, sems.at[i])
        for i, (source, target) in enumerate(zip(sources, targets))
    ]
    for copy in copies:
        copy.start()
    for copy in copies:
        copy.wait()
    col = lax.axis_index("col")
    for i, k in enumerate(served):
        slots, _ = requests(owner_ref, slot_ref, col ^ k, col)
        for j in range(PAIR):
            slots_out[i * PAIR + j] = slots[j]
    slots, _ = requests(owner_ref, slot_ref, col, col ^ far)
    for j in range(PAIR):
        slots_out[len(served) * PAIR + j] = slots[j]
    row_out[...] = row_ref[...] * occ_ref[col]
    pot_out[...] = jnp.broadcast_to(pot_ref[...], (TW, pot_ref.shape[1])).T
    hi_out[...], lo_out[...] = split(chunk_ref[...])
    for k in range(phi_hi.shape[0]):
        places, count = requests(owner_ref, None, col, col ^ k)
        for j in range(PAIR):
            weight = jnp.where(count > j, corr_ref[col, places[j]], 0).astype(jnp.float32)
            part = phi_ref[0, :, pl.ds(pl.multiple_of(places[j] * TW, TW), TW)] * weight
            at = slice(j * TW, (j + 1) * TW)
            phi_hi[k, :, at], phi_lo[k, :, at] = split(part)


def tiles(refs, slots_ref, i):
    return [
        jnp.concatenate([tile(ref, slots_ref[i * PAIR + j]) for j in range(PAIR)], axis=0)
        for ref in refs
    ]


def density_kernel(groups, n_served, n_chunks, *refs):
    slots_ref, own_row, own_hi, own_lo, occ_ref = refs[:5]
    refs = refs[5:]
    row_refs, chunk_refs = refs[: groups - 1], refs[groups - 1 : groups - 1 + n_chunks]
    refs = refs[groups - 1 + n_chunks :]
    scaled_hi, scaled_lo = refs[:2]
    outs = refs[2 : 2 + n_served]
    scaled_ref, col_hi, col_lo = refs[2 + n_served :]
    row, col = lax.axis_index("row"), lax.axis_index("col")
    for k in range(n_chunks):
        at = place(row, chunk_refs, k)
        if k == 0 and n_chunks > 1:
            col_hi[at, :], col_lo[at, :] = own_hi[...], own_lo[...]
        else:
            col_hi[at, :], col_lo[at, :] = split(chunk_refs[k][...])
    scaled_ref[col] = own_row[...]
    for k in range(1, groups):
        scaled_ref[col ^ k] = row_refs[k - 1][...] * occ_ref[col ^ k]
    left = split(jnp.concatenate([scaled_ref[k] for k in range(groups)], axis=1))
    scaled_hi[...], scaled_lo[...] = left
    for i, out in enumerate(outs):
        out[...] = dot3(left, tiles((col_hi, col_lo), slots_ref, i))


def own_kernel(phi_hi, phi_lo, strip_ref, out_ref):
    out_ref[...] = dot3((phi_hi[0], phi_lo[0]), split(strip_ref[...]))


def final_kernel(far, others, n_chunks, *refs):
    slots_ref, phi_hi, phi_lo, rows_ref, pot_ref, own_ref, hi_ref, lo_ref = refs[:8]
    chunks, refs = refs[8 : 8 + n_chunks], refs[8 + n_chunks :]
    strips, (density_ref, potential_ref, block_ref) = refs[: len(others)], refs[len(others) :]
    row = lax.axis_index("row")
    for k in range(n_chunks):
        block_ref[place(row, chunks, k), :] = chunks[k][...]
    columns = tiles((block_ref,), slots_ref, len(others) + 1)[0]
    strip = dot3((hi_ref[...], lo_ref[...]), split(columns))
    coupled = own_ref[...] + dot3((phi_hi[far], phi_lo[far]), split(strip))
    for k, strip_ref in zip(others, strips):
        coupled += dot3((phi_hi[k], phi_lo[k]), split(strip_ref[...]))
    field = rows_ref[0] * coupled
    weights = pot_ref[...]
    parts = [field[:, at : at + TW] for at in range(0, field.shape[1], TW)]
    for at, part in enumerate(parts):
        potential_ref[:, at * TW : (at + 1) * TW] = jnp.sum(part * weights, axis=0, keepdims=True)
    ones = jnp.ones((8, TW), jnp.bfloat16)
    density_ref[...] = sum(
        lax.dot_general(ones, part, NT, preferred_element_type=jnp.float32)
        for part in split(sum(parts))
    )[:1]


def call(kernel, in_specs, outs, scratch=(), flops=0):
    out_specs = [SMEM if len(o.shape) == 1 else VMEM for o in outs]
    return pl.pallas_call(
        kernel,
        out_shape=outs,
        in_specs=in_specs,
        out_specs=out_specs,
        scratch_shapes=list(scratch),
        compiler_params=PARAMS,
        cost_estimate=pl.CostEstimate(flops=flops, bytes_accessed=2 << 20, transcendentals=0),
    )


def per_device(
    row_vectors,
    column_vectors,
    occupation,
    phi_row,
    phi_col,
    potential,
    tile_owner,
    tile_slot,
    correlation,
):
    groups = lax.axis_size("col")
    rows, quarter = row_vectors.shape
    states = occupation.shape[0]
    points = phi_col.shape[1]
    width = PAIR * TW
    block = column_vectors.shape[0] * lax.axis_size("row")
    far = groups // 2
    others = [k for k in range(groups - 1, 0, -1) if k != far]
    served = others + [0]
    f32 = lambda *shape: jax.ShapeDtypeStruct(shape, jnp.float32)
    bf16 = lambda *shape: jax.ShapeDtypeStruct(shape, jnp.bfloat16)
    row_pieces = gather_rows(row_vectors)
    chunks = gather_columns(column_vectors)
    crossed = flip(column_vectors, "col", far)
    far_chunks = gather_columns(crossed)
    slots, own_row, own_hi, own_lo, occ, phi_hi, phi_lo, pot = call(
        functools.partial(prepare_kernel, served, far),
        [HBM] * 8,
        [
            jax.ShapeDtypeStruct(((len(served) + 1) * PAIR,), jnp.int32),
            f32(rows, quarter),
            bf16(*column_vectors.shape),
            bf16(*column_vectors.shape),
            f32(groups, 1, quarter),
            bf16(groups, points, width),
            bf16(groups, points, width),
            f32(points, TW),
        ],
        [pltpu.SMEM(tile_owner.shape, jnp.int32)] * 3
        + [pltpu.VMEM(a.shape, jnp.float32) for a in (row_vectors, column_vectors, phi_col, potential)]
        + [pltpu.SemaphoreType.DMA((8,))],
    )(
        *(
            pltpu.with_memory_space_constraint(a, pltpu.HBM)
            for a in (
                tile_owner,
                tile_slot,
                correlation,
                row_vectors,
                column_vectors,
                occupation.reshape(groups, 1, quarter),
                phi_col,
                potential,
            )
        )
    )
    if len(chunks) > 1:
        chunks[0] = own_hi
    scaled_hi, scaled_lo, *strips = call(
        functools.partial(density_kernel, groups, len(served), len(chunks)),
        [SMEM] + [VMEM] * (3 + groups + len(chunks)),
        [bf16(rows, states)] * 2 + [f32(rows, width)] * len(served),
        [
            pltpu.VMEM((groups, rows, quarter), jnp.float32),
            pltpu.VMEM((block, states), jnp.bfloat16),
            pltpu.VMEM((block, states), jnp.bfloat16),
        ],
        6 * rows * width * states * len(served),
    )(slots, own_row, own_hi, own_lo, occ, *row_pieces[1:], *chunks)
    strips = dict(zip(served, strips))
    arrived = [flip(strips[k], "col", k) for k in others]
    own = call(own_kernel, [VMEM] * 3, [f32(points, rows)], (), 6 * points * rows * width)(
        phi_hi, phi_lo, strips[0]
    )[0]
    return tuple(
        call(
            functools.partial(final_kernel, far, others, len(far_chunks)),
            [SMEM] + [VMEM] * (7 + len(far_chunks) + len(others)),
            [f32(1, points), f32(1, rows)],
            [pltpu.VMEM((block, states), jnp.float32)],
        )(slots, phi_hi, phi_lo, phi_row, pot, own, scaled_hi, scaled_lo, *far_chunks, *arrived)
    )


def solution(mesh):
    in_specs = (
        P("row", "col"),
        P(("col", "row"), None),
        P(),
        P(("row", "col"), None, None),
        P(("row", "col"), None, None),
        P(("row", "col"), None),
        P("row", None),
        P("row", None),
        P("row", None),
    )
    out_specs = (P(("row", "col"), None), P(("row", "col"), None))

    return jax.shard_map(
        per_device, mesh=mesh, in_specs=in_specs, out_specs=out_specs, check_vma=False
    )
```

time: 120 us -> 51.7 us (0.43)
  waiting for transfers between devices: 74 us -> 24 us
  starting transfers between devices: 0.08 us -> 19.8 us
  blocking collectives: 17.7 us -> 0 us
  between operations: 14.1 us -> 0.7 us
  matrix products: 7.11 us -> 0 us
  Pallas kernels: 0 us -> 7.01 us
  local copies, waits for them, and re-layouts: 5.14 us -> 0.01 us
  other arithmetic: 1.41 us -> 0 us
    all_gather x2 -> x0, waiting for transfers between devices: 73.3 us -> none  [the longest x1 60.8 us: per_device(): strip_row = lax.all_gather(density_block, 'col', axis=1, tiled=True)]
    ppermute x0 -> x20, waiting for transfers between devices: none -> 24 us  [flip(): return lax.ppermute(x, axis, [(i, i ^ bit) for i in range(size)])]
    ppermute x0 -> x20, starting transfers between devices: none -> 19.8 us  [flip(): return lax.ppermute(x, axis, [(i, i ^ bit) for i in range(size)])]
    all_gather x1 -> x0, blocking collectives: 17.7 us -> none  [per_device(): states = lax.all_gather(row_vectors, 'col', axis=1, tiled=True)]
    dot_general x2 -> x0, matrix products: 7.11 us -> none  [the longest x1 3.8 us: per_device(): lax.dot_general(scaled, lax.all_gather(column_vectors, 'row', axis=0, til...]
    pallas_call x0 -> x4, Pallas kernels: none -> 7.01 us  [the longest x1 2.64 us: per_device(): call(functools.partial(final_kernel, far, others, len(far_chunks)), [SMEM...]
    reshape x1 -> x0, local copies, waits for them, and re-layouts: 2.24 us -> none  [per_device(): all_tiles = strip_row.reshape(row_count, groups * TPD, TW)]
    gather x1 -> x0, local copies, waits for them, and re-layouts: 1.59 us -> none  [per_device(): jnp.take(all_tiles, owners * TPD + slots, axis=1) * weights[None, :, None]]
  transfers between devices with their start and end apart: 2 -> 20, of which waited for: 2 -> 8; matrix products, arithmetic and copies ran while one was open for 2% -> 0% of each run, Pallas kernels for 0% -> 8%
where the time goes in v1:
time: 51.7 us; the launch traced here: 51.6 us
  waiting for transfers between devices  24 us (46%)
  starting transfers between devices  19.8 us (38%)
  Pallas kernels  7.01 us (14%)
  between operations  0.7 us (1%)
    ppermute x20, waiting for transfers between devices, flip(): return lax.ppermute(x, axis, [(i, i ^ bit) for i in range(size)])  24 us
    ppermute x20, starting transfers between devices, flip(): return lax.ppermute(x, axis, [(i, i ^ bit) for i in range(size)])  19.8 us
    pallas_call x1, Pallas kernels, per_device(): call(functools.partial(final_kernel, far, others, len(far_chunks)), [SMEM...  2.64 us
    pallas_call x1, Pallas kernels, per_device(): call(functools.partial(prepare_kernel, served, far), [HBM] * 8, [jax.Shap...  2.41 us
    pallas_call x1, Pallas kernels, per_device(): call(functools.partial(density_kernel, groups, len(served), len(chunks)),...  1.67 us
  transfers between devices with their start and end apart: 20, of which 8 were waited for; matrix products, arithmetic and copies ran while one was open for 0% of the time, Pallas kernels for 8%

profile of v1, /device:TPU:0, one launch (start us, length us, event | category | flops | bytes accessed | tf_op | source)
XLA Modules:
  0.0 51.6 jit_solution(4552032854165127022)
XLA Ops:
  0.6 3.1 %collective-permute-start = (f32[256,128]{1,0:T(8,128)}, f32[256,128]{1,0:T(8,128)S(1)}, u32[]{:S(2)}, u32[]{:S(2)}) collective-permute-start(f32[256,128]{1,0:T(8,128)} %refs_3_.2), channel_id=1, source_target_pairs={{0,1},{1,0},{2,3},{3,2},{4,5},{5,4},{6,7},{7,6},{8,9},{9,8},{10,11... | collective-permute-start | bytes 393224 | tf_op jit(solution)/shard_map/ppermute | solution.py:35
  3.8 1.5 %collective-permute-start.4 = (f32[96,512]{1,0:T(8,128)}, f32[96,512]{1,0:T(8,128)S(1)}, u32[]{:S(2)}, u32[]{:S(2)}) collective-permute-start(f32[96,512]{1,0:T(8,128)} %refs_4_.1), channel_id=1, source_target_pairs={{0,8},{4,12},{8,0},{12,4},{16,24},{20,28},{24,16},{28,20},{1,9},{5... | collective-permute-start | bytes 589832 | tf_op jit(solution)/shard_map/ppermute | solution.py:35
  5.2 1.5 %collective-permute-start.6 = (f32[96,512]{1,0:T(8,128)}, f32[96,512]{1,0:T(8,128)S(1)}, u32[]{:S(2)}, u32[]{:S(2)}) collective-permute-start(f32[96,512]{1,0:T(8,128)} %refs_4_.1), channel_id=1, source_target_pairs={{0,16},{4,20},{8,24},{12,28},{16,0},{20,4},{24,8},{28,12},{1,17},{... | collective-permute-start | bytes 589832 | tf_op jit(solution)/shard_map/ppermute | solution.py:35
  6.8 2.6 %collective-permute-start.1 = (f32[256,128]{1,0:T(8,128)}, f32[256,128]{1,0:T(8,128)S(1)}, u32[]{:S(2)}, u32[]{:S(2)}) collective-permute-start(f32[256,128]{1,0:T(8,128)} %refs_3_.2), channel_id=1, source_target_pairs={{0,2},{1,3},{2,0},{3,1},{4,6},{5,7},{6,4},{7,5},{8,10},{9,11},{10,... | collective-permute-start | bytes 393224 | tf_op jit(solution)/shard_map/ppermute | solution.py:35
  9.4 0.0 collective-permute-start.3
  9.4 0.0 collective-permute-done.refs_5_
  9.4 1.8 %collective-permute-start.8 = (f32[96,512]{1,0:T(8,128)}, f32[96,512]{1,0:T(8,128)S(1)}, u32[]{:S(2)}, u32[]{:S(2)}) collective-permute-start(f32[96,512]{1,0:T(8,128)} %refs_4_.1), channel_id=1, source_target_pairs={{0,24},{4,28},{8,16},{12,20},{16,8},{20,12},{24,0},{28,4},{1,25},{... | collective-permute-start | bytes 589832 | tf_op jit(solution)/shard_map/ppermute | solution.py:35
  11.1 3.9 %collective-permute-done.1.refs_6_ = f32[256,128]{1,0:T(8,128)S(1)} collective-permute-done((f32[256,128]{1,0:T(8,128)}, f32[256,128]{1,0:T(8,128)S(1)}, u32[]{:S(2)}, u32[]{:S(2)}) %collective-permute-start.1) | collective-permute-done | bytes 131104 | tf_op jit(solution)/shard_map/ppermute | solution.py:35
  15.0 0.5 collective-permute-start.10
  15.5 0.0 collective-permute-done.4.refs_10_
  15.5 0.0 collective-permute-start.5
  15.5 0.0 collective-permute-done.6.refs_12_
  15.5 0.5 collective-permute-start.7
  16.0 0.0 collective-permute-done.3.refs_9_
  16.1 2.6 %collective-permute-start.2 = (f32[256,128]{1,0:T(8,128)S(1)}, f32[256,128]{1,0:T(8,128)S(1)}, u32[]{:S(2)}, u32[]{:S(2)}) collective-permute-start(f32[256,128]{1,0:T(8,128)S(1)} %collective-permute-done.1.refs_6_), channel_id=1, source_target_pairs={{0,1},{1,0},{2,3},{3,2},{4,5},{5,4},{6,7},{7,6},{8,9},{9,8},{10,11... | collective-permute-start | bytes 393224 | tf_op jit(solution)/shard_map/ppermute | solution.py:35
  18.6 0.0 collective-permute-done.8.refs_14_
  18.6 0.0 collective-permute-start.9
  18.6 7.5 %collective-permute-done.10.refs_8_ = f32[96,512]{1,0:T(8,128)S(1)} collective-permute-done((f32[96,512]{1,0:T(8,128)}, f32[96,512]{1,0:T(8,128)S(1)}, u32[]{:S(2)}, u32[]{:S(2)}) %collective-permute-start.10) | collective-permute-done | bytes 196640 | tf_op jit(solution)/shard_map/ppermute | solution.py:35
  26.1 0.0 collective-permute-start.11
  26.1 0.3 collective-permute-done.2.refs_7_
  26.5 0.6 %collective-permute-start.12 = (f32[96,512]{1,0:T(8,128)S(1)}, f32[96,512]{1,0:T(8,128)S(1)}, u32[]{:S(2)}, u32[]{:S(2)}) collective-permute-start(f32[96,512]{1,0:T(8,128)S(1)} %collective-permute-done.10.refs_8_), channel_id=1, source_target_pairs={{0,8},{4,12},{8,0},{12,4},{16,24},{20,28},{24,16},{28,20},{1,9},{5... | collective-permute-start | bytes 589832 | tf_op jit(solution)/shard_map/ppermute | solution.py:35
  27.1 0.0 collective-permute-done.5.refs_11_
  27.1 0.0 collective-permute-start.14
  27.1 0.0 collective-permute-done.7.refs_13_
  27.1 2.9 %collective-permute-start.16 = (f32[96,512]{1,0:T(8,128)S(1)}, f32[96,512]{1,0:T(8,128)S(1)}, u32[]{:S(2)}, u32[]{:S(2)}) collective-permute-start(f32[96,512]{1,0:T(8,128)S(1)} %collective-permute-done.10.refs_8_), channel_id=1, source_target_pairs={{0,24},{4,28},{8,16},{12,20},{16,8},{20,12},{24,0},{28,4},{1,25},{... | collective-permute-start | bytes 589832 | tf_op jit(solution)/shard_map/ppermute | solution.py:35
  30.0 2.4 %shard_map.104 = (s32[8]{0:T(128)S(1)}, f32[256,128]{1,0:T(8,128)S(1)}, bf16[96,512]{1,0:T(8,128)(2,1)S(1)}, bf16[96,512]{1,0:T(8,128)(2,1)S(1)}, f32[4,1,128]{2...) custom-call(s32[4,8]{1,0:T(4,128)} %refs_0_.1, ...), custom_call_target="tpu_custom_call" | custom-call | bytes 2097152 | tf_op jit(solution)/shard_map/pallas_call | solution.py:213
  32.4 0.0 collective-permute-done.9.refs_15_
  32.4 1.7 %shard_map.105 = (bf16[256,512]{1,0:T(8,128)(2,1)S(1)}, bf16[256,512]{1,0:T(8,128)(2,1)S(1)}, f32[256,256]{1,0:T(8,128)S(1)}, f32[256,256]{1,0:T(8,128)S(1)}, f32[256,256]{1,0:T(8,128)S(1)}) custom-call(s32[8]{0:T(128)S(1)} %get-tuple-element.15.refs_0_, f32[256,128]{1,0:T(8,128)S(1)} %get-tuple-element.19.refs_1_, ...), custom_call_target="tpu_custom_call" | custom-call | flops 603979776 | bytes 2097152 | tf_op jit(solution)/shard_map/pallas_call | solution.py:246
  34.1 1.7 %collective-permute-start.18 = (f32[256,256]{1,0:T(8,128)S(1)}, f32[256,256]{1,0:T(8,128)S(1)}, u32[]{:S(2)}, u32[]{:S(2)}) collective-permute-start(f32[256,256]{1,0:T(8,128)S(1)} %get-tuple-element.26), channel_id=1, source_target_pairs={{0,3},{1,2},{2,1},{3,0},{4,7},{5,6},{6,5},{7,4},{8,11},{9,10},{10,... | collective-permute-start | bytes 786440 | tf_op jit(solution)/shard_map/ppermute | solution.py:35
  35.8 0.0 collective-permute-done.11.refs_9_
  35.8 0.0 collective-permute-start.19
  35.8 0.0 collective-permute-done.12.refs_10_
  35.8 0.1 collective-permute-start.13
  35.8 2.2 %collective-permute-done.14.refs_12_ = f32[96,512]{1,0:T(8,128)S(1)} collective-permute-done((f32[96,512]{1,0:T(8,128)S(1)}, f32[96,512]{1,0:T(8,128)S(1)}, u32[]{:S(2)}, u32[]{:S(2)}) %collective-permute-start.14) | collective-permute-done | bytes 196640 | tf_op jit(solution)/shard_map/ppermute | solution.py:35
  38.0 0.0 collective-permute-start.15
  38.0 0.0 collective-permute-done.16.refs_14_
  38.0 0.5 collective-permute-start.17
  38.5 0.0 copy-start
  38.5 0.3 shard_map.106.refs_5_
  38.9 0.0 collective-permute-done.13.refs_11_
  38.9 0.6 %collective-permute-done.15.refs_13_ = f32[96,512]{1,0:T(8,128)S(1)} collective-permute-done((f32[96,512]{1,0:T(8,128)S(1)}, f32[96,512]{1,0:T(8,128)S(1)}, u32[]{:S(2)}, u32[]{:S(2)}) %collective-permute-start.15) | collective-permute-done | bytes 196640 | tf_op jit(solution)/shard_map/ppermute | solution.py:35
  39.5 0.3 collective-permute-done.17.refs_15_
  39.8 5.4 %collective-permute-done.18.refs_16_ = f32[256,256]{1,0:T(8,128)S(1)} collective-permute-done((f32[256,256]{1,0:T(8,128)S(1)}, f32[256,256]{1,0:T(8,128)S(1)}, u32[]{:S(2)}, u32[]{:S(2)}) %collective-permute-start.18) | collective-permute-done | bytes 262176 | tf_op jit(solution)/shard_map/ppermute | solution.py:35
  45.1 3.8 %collective-permute-done.19.refs_17_ = f32[256,256]{1,0:T(8,128)S(1)} collective-permute-done((f32[256,256]{1,0:T(8,128)S(1)}, f32[256,256]{1,0:T(8,128)S(1)}, u32[]{:S(2)}, u32[]{:S(2)}) %collective-permute-start.19) | collective-permute-done | bytes 262176 | tf_op jit(solution)/shard_map/ppermute | solution.py:35
  48.9 0.0 copy-done
  48.9 2.6 %shard_map.107 = (f32[1,256]{1,0:T(1,128)}, f32[1,256]{1,0:T(1,128)}) custom-call(s32[8]{0:T(128)S(1)} %get-tuple-element.15.refs_0_, bf16[4,256,256]{2,1,0:T(8,128)(2,1)S(1)} %get-tuple-element.16.phi_hi.refs_1_, bf16[4,256,256]{2,1,0:T(8,128)(2,1)S(1)} %get-tuple-element.17.phi_lo.refs_2_, f32[1,256,256]{2,1,0:T(8,128)S(1)} %copy-done, ...), custom_call_target="tpu_custom_call" | custom-call | bytes 2097152 | tf_op jit(solution)/shard_map/pallas_call | solution.py:263
Async XLA Ops:
  0.6 8.7 %collective-permute-start = (f32[256,128]{1,0:T(8,128)}, f32[256,128]{1,0:T(8,128)S(1)}, u32[]{:S(2)}, u32[]{:S(2)}) collective-permute-start(f32[256,128]{1,0:T(8,128)} %refs_3_.2), channel_id=1, source_target_pairs={{0,1},{1,0},{2,3},{3,2},{4,5},{5,4},{6,7},{7,6},{8,9},{9,8},{10,11... | collective-permute-start | bytes 393224 | tf_op jit(solution)/shard_map/ppermute | solution.py:35
  3.8 11.8 %collective-permute-start.4 = (f32[96,512]{1,0:T(8,128)}, f32[96,512]{1,0:T(8,128)S(1)}, u32[]{:S(2)}, u32[]{:S(2)}) collective-permute-start(f32[96,512]{1,0:T(8,128)} %refs_4_.1), channel_id=1, source_target_pairs={{0,8},{4,12},{8,0},{12,4},{16,24},{20,28},{24,16},{28,20},{1,9},{5... | collective-permute-start | bytes 589832 | tf_op jit(solution)/shard_map/ppermute | solution.py:35
  5.2 10.3 %collective-permute-start.6 = (f32[96,512]{1,0:T(8,128)}, f32[96,512]{1,0:T(8,128)S(1)}, u32[]{:S(2)}, u32[]{:S(2)}) collective-permute-start(f32[96,512]{1,0:T(8,128)} %refs_4_.1), channel_id=1, source_target_pairs={{0,16},{4,20},{8,24},{12,28},{16,0},{20,4},{24,8},{28,12},{1,17},{... | collective-permute-start | bytes 589832 | tf_op jit(solution)/shard_map/ppermute | solution.py:35
  6.8 8.3 %collective-permute-start.1 = (f32[256,128]{1,0:T(8,128)}, f32[256,128]{1,0:T(8,128)S(1)}, u32[]{:S(2)}, u32[]{:S(2)}) collective-permute-start(f32[256,128]{1,0:T(8,128)} %refs_3_.2), channel_id=1, source_target_pairs={{0,2},{1,3},{2,0},{3,1},{4,6},{5,7},{6,4},{7,5},{8,10},{9,11},{10,... | collective-permute-start | bytes 393224 | tf_op jit(solution)/shard_map/ppermute | solution.py:35
  9.4 6.7 %collective-permute-start.3 = (f32[96,512]{1,0:T(8,128)}, f32[96,512]{1,0:T(8,128)S(1)}, u32[]{:S(2)}, u32[]{:S(2)}) collective-permute-start(f32[96,512]{1,0:T(8,128)} %refs_4_.1), channel_id=1, source_target_pairs={{0,4},{4,0},{8,12},{12,8},{16,20},{20,16},{24,28},{28,24},{1,5},{5... | collective-permute-start | bytes 589832 | tf_op jit(solution)/shard_map/ppermute | solution.py:35
  9.4 9.3 %collective-permute-start.8 = (f32[96,512]{1,0:T(8,128)}, f32[96,512]{1,0:T(8,128)S(1)}, u32[]{:S(2)}, u32[]{:S(2)}) collective-permute-start(f32[96,512]{1,0:T(8,128)} %refs_4_.1), channel_id=1, source_target_pairs={{0,24},{4,28},{8,16},{12,20},{16,8},{20,12},{24,0},{28,4},{1,25},{... | collective-permute-start | bytes 589832 | tf_op jit(solution)/shard_map/ppermute | solution.py:35
  15.0 11.1 %collective-permute-start.10 = (f32[96,512]{1,0:T(8,128)}, f32[96,512]{1,0:T(8,128)S(1)}, u32[]{:S(2)}, u32[]{:S(2)}) collective-permute-start(f32[96,512]{1,0:T(8,128)} %refs_4_.1), channel_id=1, source_target_pairs={{0,2},{1,3},{2,0},{3,1},{4,6},{5,7},{6,4},{7,5},{8,10},{9,11},{10,... | collective-permute-start | bytes 589832 | tf_op jit(solution)/shard_map/ppermute | solution.py:35
  15.5 11.5 %collective-permute-start.5 = (f32[96,512]{1,0:T(8,128)S(1)}, f32[96,512]{1,0:T(8,128)S(1)}, u32[]{:S(2)}, u32[]{:S(2)}) collective-permute-start(f32[96,512]{1,0:T(8,128)S(1)} %collective-permute-done.4.refs_10_), channel_id=1, source_target_pairs={{0,4},{4,0},{8,12},{12,8},{16,20},{20,16},{24,28},{28,24},{1,5},{5... | collective-permute-start | bytes 589832 | tf_op jit(solution)/shard_map/ppermute | solution.py:35
  15.5 11.5 %collective-permute-start.7 = (f32[96,512]{1,0:T(8,128)S(1)}, f32[96,512]{1,0:T(8,128)S(1)}, u32[]{:S(2)}, u32[]{:S(2)}) collective-permute-start(f32[96,512]{1,0:T(8,128)S(1)} %collective-permute-done.6.refs_12_), channel_id=1, source_target_pairs={{0,4},{4,0},{8,12},{12,8},{16,20},{20,16},{24,28},{28,24},{1,5},{5... | collective-permute-start | bytes 589832 | tf_op jit(solution)/shard_map/ppermute | solution.py:35
  16.1 10.4 %collective-permute-start.2 = (f32[256,128]{1,0:T(8,128)S(1)}, f32[256,128]{1,0:T(8,128)S(1)}, u32[]{:S(2)}, u32[]{:S(2)}) collective-permute-start(f32[256,128]{1,0:T(8,128)S(1)} %collective-permute-done.1.refs_6_), channel_id=1, source_target_pairs={{0,1},{1,0},{2,3},{3,2},{4,5},{5,4},{6,7},{7,6},{8,9},{9,8},{10,11... | collective-permute-start | bytes 393224 | tf_op jit(solution)/shard_map/ppermute | solution.py:35
  18.6 13.8 %collective-permute-start.9 = (f32[96,512]{1,0:T(8,128)S(1)}, f32[96,512]{1,0:T(8,128)S(1)}, u32[]{:S(2)}, u32[]{:S(2)}) collective-permute-start(f32[96,512]{1,0:T(8,128)S(1)} %collective-permute-done.8.refs_14_), channel_id=1, source_target_pairs={{0,4},{4,0},{8,12},{12,8},{16,20},{20,16},{24,28},{28,24},{1,5},{5... | collective-permute-start | bytes 589832 | tf_op jit(solution)/shard_map/ppermute | solution.py:35
  26.1 9.6 %collective-permute-start.11 = (f32[96,512]{1,0:T(8,128)S(1)}, f32[96,512]{1,0:T(8,128)S(1)}, u32[]{:S(2)}, u32[]{:S(2)}) collective-permute-start(f32[96,512]{1,0:T(8,128)S(1)} %collective-permute-done.10.refs_8_), channel_id=1, source_target_pairs={{0,4},{4,0},{8,12},{12,8},{16,20},{20,16},{24,28},{28,24},{1,5},{5... | collective-permute-start | bytes 589832 | tf_op jit(solution)/shard_map/ppermute | solution.py:35
  26.5 9.3 %collective-permute-start.12 = (f32[96,512]{1,0:T(8,128)S(1)}, f32[96,512]{1,0:T(8,128)S(1)}, u32[]{:S(2)}, u32[]{:S(2)}) collective-permute-start(f32[96,512]{1,0:T(8,128)S(1)} %collective-permute-done.10.refs_8_), channel_id=1, source_target_pairs={{0,8},{4,12},{8,0},{12,4},{16,24},{20,28},{24,16},{28,20},{1,9},{5... | collective-permute-start | bytes 589832 | tf_op jit(solution)/shard_map/ppermute | solution.py:35
  27.1 11.0 %collective-permute-start.14 = (f32[96,512]{1,0:T(8,128)S(1)}, f32[96,512]{1,0:T(8,128)S(1)}, u32[]{:S(2)}, u32[]{:S(2)}) collective-permute-start(f32[96,512]{1,0:T(8,128)S(1)} %collective-permute-done.10.refs_8_), channel_id=1, source_target_pairs={{0,16},{4,20},{8,24},{12,28},{16,0},{20,4},{24,8},{28,12},{1,17},{... | collective-permute-start | bytes 589832 | tf_op jit(solution)/shard_map/ppermute | solution.py:35
  27.1 11.0 %collective-permute-start.16 = (f32[96,512]{1,0:T(8,128)S(1)}, f32[96,512]{1,0:T(8,128)S(1)}, u32[]{:S(2)}, u32[]{:S(2)}) collective-permute-start(f32[96,512]{1,0:T(8,128)S(1)} %collective-permute-done.10.refs_8_), channel_id=1, source_target_pairs={{0,24},{4,28},{8,16},{12,20},{16,8},{20,12},{24,0},{28,4},{1,25},{... | collective-permute-start | bytes 589832 | tf_op jit(solution)/shard_map/ppermute | solution.py:35
  34.1 11.0 %collective-permute-start.18 = (f32[256,256]{1,0:T(8,128)S(1)}, f32[256,256]{1,0:T(8,128)S(1)}, u32[]{:S(2)}, u32[]{:S(2)}) collective-permute-start(f32[256,256]{1,0:T(8,128)S(1)} %get-tuple-element.26), channel_id=1, source_target_pairs={{0,3},{1,2},{2,1},{3,0},{4,7},{5,6},{6,5},{7,4},{8,11},{9,10},{10,... | collective-permute-start | bytes 786440 | tf_op jit(solution)/shard_map/ppermute | solution.py:35
  35.8 13.2 %collective-permute-start.19 = (f32[256,256]{1,0:T(8,128)S(1)}, f32[256,256]{1,0:T(8,128)S(1)}, u32[]{:S(2)}, u32[]{:S(2)}) collective-permute-start(f32[256,256]{1,0:T(8,128)S(1)} %get-tuple-element.27), channel_id=1, source_target_pairs={{0,1},{1,0},{2,3},{3,2},{4,5},{5,4},{6,7},{7,6},{8,9},{9,8},{10,11... | collective-permute-start | bytes 786440 | tf_op jit(solution)/shard_map/ppermute | solution.py:35
  35.8 3.1 %collective-permute-start.13 = (f32[96,512]{1,0:T(8,128)S(1)}, f32[96,512]{1,0:T(8,128)S(1)}, u32[]{:S(2)}, u32[]{:S(2)}) collective-permute-start(f32[96,512]{1,0:T(8,128)S(1)} %collective-permute-done.12.refs_10_), channel_id=1, source_target_pairs={{0,4},{4,0},{8,12},{12,8},{16,20},{20,16},{24,28},{28,24},{1,5},{5... | collective-permute-start | bytes 589832 | tf_op jit(solution)/shard_map/ppermute | solution.py:35
  38.0 1.4 %collective-permute-start.15 = (f32[96,512]{1,0:T(8,128)S(1)}, f32[96,512]{1,0:T(8,128)S(1)}, u32[]{:S(2)}, u32[]{:S(2)}) collective-permute-start(f32[96,512]{1,0:T(8,128)S(1)} %collective-permute-done.14.refs_12_), channel_id=1, source_target_pairs={{0,4},{4,0},{8,12},{12,8},{16,20},{20,16},{24,28},{28,24},{1,5},{5... | collective-permute-start | bytes 589832 | tf_op jit(solution)/shard_map/ppermute | solution.py:35
  38.0 1.7 %collective-permute-start.17 = (f32[96,512]{1,0:T(8,128)S(1)}, f32[96,512]{1,0:T(8,128)S(1)}, u32[]{:S(2)}, u32[]{:S(2)}) collective-permute-start(f32[96,512]{1,0:T(8,128)S(1)} %collective-permute-done.16.refs_14_), channel_id=1, source_target_pairs={{0,4},{4,0},{8,12},{12,8},{16,20},{20,16},{24,28},{28,24},{1,5},{5... | collective-permute-start | bytes 589832 | tf_op jit(solution)/shard_map/ppermute | solution.py:35
  38.5 10.4 %copy-start = (f32[1,256,256]{2,1,0:T(8,128)S(1)}, f32[1,256,256]{2,1,0:T(8,128)}, u32[]{:S(2)}) copy-start(f32[1,256,256]{2,1,0:T(8,128)} %refs_3_.3) | copy-start | bytes 786436

commit v2 on v1

v2 whole, which is shorter than its diff:
```python
import functools

import jax
import jax.numpy as jnp
from jax import lax
from jax.experimental import pallas as pl
from jax.experimental.pallas import tpu as pltpu
from jax.sharding import PartitionSpec as P


TW = 128
PAIR = 2
NT = (((1,), (1,)), ((), ()))
PARAMS = pltpu.CompilerParams(vmem_limit_bytes=16 << 20)
VMEM = pl.BlockSpec(memory_space=pltpu.VMEM)
HBM = pl.BlockSpec(memory_space=pltpu.HBM)
SMEM = pl.BlockSpec(memory_space=pltpu.SMEM)


def split(x):
    high = x.astype(jnp.bfloat16)
    return high, (x - high.astype(jnp.float32)).astype(jnp.bfloat16)


def dot3(a, b):
    (ah, al), (bh, bl) = a, b
    one = functools.partial(
        lax.dot_general, dimension_numbers=NT, preferred_element_type=jnp.float32
    )
    return one(ah, bh) + (one(ah, bl) + one(al, bh))


def flip(x, axis, bit):
    size = lax.axis_size(axis)
    return lax.ppermute(x, axis, [(i, i ^ bit) for i in range(size)])


def gather_rows(x):
    pieces = {0: x}
    bit = lax.axis_size("col") // 2
    while bit:
        for k, v in list(pieces.items()):
            pieces[k ^ bit] = flip(v, "col", bit)
        bit //= 2
    return [pieces[k] for k in range(len(pieces))]


def gather_columns(x):
    if lax.axis_size("row") != 8:
        return [lax.all_gather(x, "row", axis=0, tiled=True)]
    pieces = {0: x}
    for far in (2, 4, 6):
        pieces[far] = flip(x, "row", far)
    for near in (0, 2, 4, 6):
        pieces[near ^ 1] = flip(pieces[near], "row", 1)
    return [pieces[k] for k in range(8)]


def place(row, k, pieces):
    size = pieces[k].shape[0]
    if len(pieces) == 1:
        return pl.ds(0, size)
    return pl.ds(pl.multiple_of((row ^ k) * size, 16), size)


def requests(owner_ref, values_ref, batch, holder):
    found = [jnp.int32(0)] * PAIR
    count = jnp.int32(0)
    for t in range(owner_ref.shape[1]):
        hit = owner_ref[batch, t] == holder
        value = values_ref[batch, t] if values_ref is not None else jnp.int32(t)
        for k in range(PAIR):
            found[k] = jnp.where(hit & (count == k), value, found[k])
        count = count + hit.astype(jnp.int32)
    return found, count


def tile(ref, slot):
    return ref[pl.ds(pl.multiple_of(slot * TW, TW), TW), :]


def start_copies(sources, targets, sems):
    copies = [
        pltpu.make_async_copy(source, target, sems.at[i])
        for i, (source, target) in enumerate(zip(sources, targets))
    ]
    for copy in copies:
        copy.start()
    return copies


def basis_kernel(*refs):
    sources, refs = refs[:5], refs[5:]
    phi_hi, phi_lo, pot_out, rows_out, owner_ref, corr_ref, phi_ref, pot_ref, sems = refs
    targets = owner_ref, corr_ref, phi_ref, pot_ref, rows_out
    copies = start_copies(sources, targets, sems)
    for copy in copies[:-1]:
        copy.wait()
    col = lax.axis_index("col")
    pot_out[...] = jnp.broadcast_to(pot_ref[...], (TW, pot_ref.shape[1])).T
    for k in range(phi_hi.shape[0]):
        places, count = requests(owner_ref, None, col, col ^ k)
        for j in range(PAIR):
            weight = jnp.where(count > j, corr_ref[col, places[j]], 0).astype(jnp.float32)
            part = phi_ref[0, :, pl.ds(pl.multiple_of(places[j] * TW, TW), TW)] * weight
            at = slice(j * TW, (j + 1) * TW)
            phi_hi[k, :, at], phi_lo[k, :, at] = split(part)
    copies[-1].wait()


def tiles(refs, slots_ref, i):
    return [
        jnp.concatenate([tile(ref, slots_ref[i * PAIR + j]) for j in range(PAIR)], axis=0)
        for ref in refs
    ]


def tables_kernel(served, far, *refs):
    sources, refs = refs[:5], refs[5:]
    slots_ref, occ_ref, own_row, own_hi, own_lo = refs[:5]
    row_ref, chunk_ref, owner_ref, slot_ref, sems = refs[5:]
    targets = owner_ref, slot_ref, occ_ref, row_ref, chunk_ref
    for copy in start_copies(sources, targets, sems):
        copy.wait()
    col = lax.axis_index("col")
    for i, k in enumerate(served):
        slots, _ = requests(owner_ref, slot_ref, col ^ k, col)
        for j in range(PAIR):
            slots_ref[i * PAIR + j] = slots[j]
    slots, _ = requests(owner_ref, slot_ref, col, col ^ far)
    for j in range(PAIR):
        slots_ref[len(served) * PAIR + j] = slots[j]
    own_hi[...], own_lo[...] = split(chunk_ref[...])
    own_row[...] = row_ref[...] * occ_ref[col]


def early_kernel(groups, n_served, n_chunks, slots_ref, occ_ref, own_row, own_hi, own_lo, *refs):
    row_refs, refs = refs[: groups - 2], refs[groups - 2 :]
    chunk_refs, refs = refs[:n_chunks], refs[n_chunks:]
    left_hi, left_lo, partial_ref, last_hi, last_lo, scaled_ref, col_hi, col_lo = refs
    row, col = lax.axis_index("row"), lax.axis_index("col")
    last = col ^ (groups - 1)
    for k in range(n_chunks):
        at = place(row, k, chunk_refs)
        if k == 0 and n_chunks > 1:
            col_hi[at, :], col_lo[at, :] = own_hi[...], own_lo[...]
        else:
            col_hi[at, :], col_lo[at, :] = split(chunk_refs[k][...])
    scaled_ref[col] = own_row[...]
    for k in range(1, groups - 1):
        scaled_ref[col ^ k] = row_refs[k - 1][...] * occ_ref[col ^ k]
    scaled_ref[last] = jnp.zeros_like(own_row)
    left = split(jnp.concatenate([scaled_ref[k] for k in range(groups)], axis=1))
    left_hi[...], left_lo[...] = left
    quarter = last_hi.shape[2]
    for i in range(n_served):
        right = tiles((col_hi, col_lo), slots_ref, i)
        partial_ref[i] = dot3(left, right)
        for out, side in zip((last_hi, last_lo), right):
            out[i] = pick(side, last, quarter)


def pick(x, index, size):
    out = x[:, :size]
    for k in range(1, x.shape[1] // size):
        out = jnp.where(index == k, x[:, k * size : (k + 1) * size], out)
    return out


def density_kernel(groups, row_ref, occ_ref, partial_ref, right_hi, right_lo, *outs):
    row_hi, row_lo = outs[:2]
    left = split(row_ref[...] * occ_ref[lax.axis_index("col") ^ (groups - 1)])
    row_hi[...], row_lo[...] = left
    for i, out in enumerate(outs[2:]):
        out[...] = partial_ref[i] + dot3(left, (right_hi[i], right_lo[i]))


def own_kernel(groups, phi_hi, phi_lo, strip_ref, left_hi, left_lo, row_hi, row_lo, *outs):
    out_ref, full_hi, full_lo = outs
    out_ref[...] = dot3((phi_hi[0], phi_lo[0]), split(strip_ref[...]))
    last = lax.axis_index("col") ^ (groups - 1)
    quarter = row_hi.shape[1]
    for full, left, row in ((full_hi, left_hi, row_hi), (full_lo, left_lo, row_lo)):
        full[...] = jnp.concatenate(
            [
                jnp.where(last == k, row[...], left[:, k * quarter : (k + 1) * quarter])
                for k in range(groups)
            ],
            axis=1,
        )


def strips_kernel(others, phi_hi, phi_lo, own_ref, *refs):
    total = own_ref[...]
    for k, strip_ref in zip(others, refs):
        total += dot3((phi_hi[k], phi_lo[k]), split(strip_ref[...]))
    refs[-1][...] = total


def final_kernel(far, index, n_chunks, *refs):
    slots_ref, phi_hi, phi_lo, rows_ref, pot_ref, sum_ref, left_hi, left_lo = refs[:8]
    chunks, (density_ref, potential_ref, block_ref) = refs[8 : 8 + n_chunks], refs[8 + n_chunks :]
    row = lax.axis_index("row")
    for k in range(n_chunks):
        block_ref[place(row, k, chunks), :] = chunks[k][...]
    columns = tiles((block_ref,), slots_ref, index)[0]
    strip = dot3((left_hi[...], left_lo[...]), split(columns))
    coupled = sum_ref[...] + dot3((phi_hi[far], phi_lo[far]), split(strip))
    field = rows_ref[0] * coupled
    weights = pot_ref[...]
    parts = [field[:, at : at + TW] for at in range(0, field.shape[1], TW)]
    for at, part in enumerate(parts):
        potential_ref[:, at * TW : (at + 1) * TW] = jnp.sum(part * weights, axis=0, keepdims=True)
    ones = jnp.ones((8, TW), jnp.bfloat16)
    density_ref[...] = sum(
        lax.dot_general(ones, part, NT, preferred_element_type=jnp.float32)
        for part in split(sum(parts))
    )[:1]


def call(kernel, in_specs, outs, scratch=(), flops=0):
    out_specs = [SMEM if len(o.shape) == 1 else VMEM for o in outs]
    return pl.pallas_call(
        kernel,
        out_shape=outs,
        in_specs=in_specs,
        out_specs=out_specs,
        scratch_shapes=list(scratch),
        compiler_params=PARAMS,
        cost_estimate=pl.CostEstimate(flops=flops, bytes_accessed=2 << 20, transcendentals=0),
    )


def per_device(
    row_vectors,
    column_vectors,
    occupation,
    phi_row,
    phi_col,
    potential,
    tile_owner,
    tile_slot,
    correlation,
):
    groups = lax.axis_size("col")
    rows, quarter = row_vectors.shape
    states = occupation.shape[0]
    points = phi_col.shape[1]
    width = PAIR * TW
    block = column_vectors.shape[0] * lax.axis_size("row")
    far = groups // 2
    others = [k for k in range(groups - 1, 0, -1) if k != far]
    served = others + [0]
    f32 = lambda *shape: jax.ShapeDtypeStruct(shape, jnp.float32)
    bf16 = lambda *shape: jax.ShapeDtypeStruct(shape, jnp.bfloat16)
    row_pieces = gather_rows(row_vectors)
    chunks = gather_columns(column_vectors)
    far_chunks = gather_columns(flip(column_vectors, "col", far))
    n_served = len(served)
    in_hbm = lambda *arrays: [pltpu.with_memory_space_constraint(a, pltpu.HBM) for a in arrays]
    tables = [pltpu.SMEM(tile_owner.shape, jnp.int32)] * 2
    phi_hi, phi_lo, pot, rows_field = call(
        basis_kernel,
        [HBM] * 5,
        [bf16(groups, points, width)] * 2 + [f32(points, TW), f32(*phi_row.shape)],
        tables
        + [pltpu.VMEM(a.shape, jnp.float32) for a in (phi_col, potential)]
        + [pltpu.SemaphoreType.DMA((5,))],
    )(*in_hbm(tile_owner, correlation, phi_col, potential, phi_row))
    slots, occ, own_row, own_hi, own_lo = call(
        functools.partial(tables_kernel, served, far),
        [HBM] * 5,
        [
            jax.ShapeDtypeStruct(((n_served + 1) * PAIR,), jnp.int32),
            f32(groups, 1, quarter),
            f32(rows, quarter),
            *[bf16(*column_vectors.shape)] * 2,
        ],
        [
            pltpu.VMEM((rows, quarter), jnp.float32),
            pltpu.VMEM(column_vectors.shape, jnp.float32),
            *tables,
            pltpu.SemaphoreType.DMA((5,)),
        ],
    )(
        *in_hbm(
            tile_owner,
            tile_slot,
            occupation.reshape(groups, 1, quarter),
            row_vectors,
            column_vectors,
        )
    )
    if len(chunks) > 1:
        chunks[0] = own_hi
    left_hi, left_lo, partial, right_hi, right_lo = call(
        functools.partial(early_kernel, groups, n_served, len(chunks)),
        [SMEM] + [VMEM] * (4 + groups - 2 + len(chunks)),
        [
            *[bf16(rows, states)] * 2,
            f32(n_served, rows, width),
            *[bf16(n_served, width, quarter)] * 2,
        ],
        [
            pltpu.VMEM((groups, rows, quarter), jnp.float32),
            *[pltpu.VMEM((block, states), jnp.bfloat16)] * 2,
        ],
        6 * rows * width * states * n_served,
    )(slots, occ, own_row, own_hi, own_lo, *row_pieces[1:-1], *chunks)
    row_hi, row_lo, *strips = call(
        functools.partial(density_kernel, groups),
        [VMEM] * 5,
        [bf16(rows, quarter)] * 2 + [f32(rows, width)] * n_served,
        (),
        6 * rows * width * quarter * n_served,
    )(row_pieces[-1], occ, partial, right_hi, right_lo)
    strips = dict(zip(served, strips))
    arrived = [flip(strips[k], "col", k) for k in others]
    own, full_hi, full_lo = call(
        functools.partial(own_kernel, groups),
        [VMEM] * 7,
        [f32(points, rows)] + [bf16(rows, states)] * 2,
        (),
        6 * points * rows * width,
    )(phi_hi, phi_lo, strips[0], left_hi, left_lo, row_hi, row_lo)
    summed = call(
        functools.partial(strips_kernel, others),
        [VMEM] * (3 + len(others)),
        [f32(points, rows)],
        (),
        6 * points * rows * width * len(others),
    )(phi_hi, phi_lo, own, *arrived)[0]
    return tuple(
        call(
            functools.partial(final_kernel, far, n_served, len(far_chunks)),
            [SMEM] + [VMEM] * (7 + len(far_chunks)),
            [f32(1, points), f32(1, rows)],
            [pltpu.VMEM((block, states), jnp.float32)],
        )(slots, phi_hi, phi_lo, rows_field, pot, summed, full_hi, full_lo, *far_chunks)
    )


def solution(mesh):
    in_specs = (
        P("row", "col"),
        P(("col", "row"), None),
        P(),
        P(("row", "col"), None, None),
        P(("row", "col"), None, None),
        P(("row", "col"), None),
        P("row", None),
        P("row", None),
        P("row", None),
    )
    out_specs = (P(("row", "col"), None), P(("row", "col"), None))

    return jax.shard_map(
        per_device, mesh=mesh, in_specs=in_specs, out_specs=out_specs, check_vma=False
    )
```

time: 51.7 us -> 52.8 us (1.021)
  Pallas kernels: 7.01 us -> 8.48 us
  starting transfers between devices: 19.8 us -> 19.1 us
    pallas_call x4 -> x7, Pallas kernels: 7.01 us -> 8.48 us  [the longest x1 2.24 us: per_device(): call(functools.partial(final_kernel, far, n_served, len(far_chunks)), [SM...]
    ppermute x20, starting transfers between devices: 19.8 us -> 19.1 us  [flip(): return lax.ppermute(x, axis, [(i, i ^ bit) for i in range(size)])]
  transfers between devices with their start and end apart: 20 -> 20, of which waited for: 8 -> 6; matrix products, arithmetic and copies ran while one was open for 0% -> 0% of each run, Pallas kernels for 8% -> 12%
where the time goes in v2:
time: 52.8 us; the launch traced here: 52.6 us
  waiting for transfers between devices  24.2 us (46%)
  starting transfers between devices  19.1 us (36%)
  Pallas kernels  8.48 us (16%)
  between operations  0.76 us (1%)
    ppermute x20, waiting for transfers between devices, flip(): return lax.ppermute(x, axis, [(i, i ^ bit) for i in range(size)])  24.2 us
    ppermute x20, starting transfers between devices, flip(): return lax.ppermute(x, axis, [(i, i ^ bit) for i in range(size)])  19.1 us
    pallas_call x1, Pallas kernels, per_device(): call(functools.partial(final_kernel, far, n_served, len(far_chunks)), [SM...  2.24 us
    pallas_call x1, Pallas kernels, per_device(): call(functools.partial(tables_kernel, served, far), [HBM] * 5, [jax.Shape...  1.75 us
    pallas_call x1, Pallas kernels, per_device(): call(functools.partial(early_kernel, groups, n_served, len(chunks)), [SME...  1.67 us
    pallas_call x1, Pallas kernels, per_device(): call(basis_kernel, [HBM] * 5, [bf16(groups, points, width)] * 2 + [f32(po...  1.55 us
  transfers between devices with their start and end apart: 20, of which 6 were waited for; matrix products, arithmetic and copies ran while one was open for 0% of the time, Pallas kernels for 12%

profile of v2, /device:TPU:0, one launch (start us, length us, event | category | flops | bytes accessed | tf_op | source)
XLA Modules:
  0.0 52.6 jit_solution(6176220059975781320)
XLA Ops:
  0.6 3.0 %collective-permute-start.4 = (f32[96,512]{1,0:T(8,128)}, f32[96,512]{1,0:T(8,128)S(1)}, u32[]{:S(2)}, u32[]{:S(2)}) collective-permute-start(f32[96,512]{1,0:T(8,128)} %refs_4_.2), channel_id=1, source_target_pairs={{0,8},{4,12},{8,0},{12,4},{16,24},{20,28},{24,16},{28,20},{1,9},{5... | collective-permute-start | bytes 589832 | tf_op jit(solution)/shard_map/ppermute | solution.py:35
  3.7 1.5 %collective-permute-start.6 = (f32[96,512]{1,0:T(8,128)}, f32[96,512]{1,0:T(8,128)S(1)}, u32[]{:S(2)}, u32[]{:S(2)}) collective-permute-start(f32[96,512]{1,0:T(8,128)} %refs_4_.2), channel_id=1, source_target_pairs={{0,16},{4,20},{8,24},{12,28},{16,0},{20,4},{24,8},{28,12},{1,17},{... | collective-permute-start | bytes 589832 | tf_op jit(solution)/shard_map/ppermute | solution.py:35
  5.2 0.0 collective-permute-start.8
  5.2 3.0 %collective-permute-start = (f32[256,128]{1,0:T(8,128)}, f32[256,128]{1,0:T(8,128)S(1)}, u32[]{:S(2)}, u32[]{:S(2)}) collective-permute-start(f32[256,128]{1,0:T(8,128)} %refs_3_.2), channel_id=1, source_target_pairs={{0,2},{1,3},{2,0},{3,1},{4,6},{5,7},{6,4},{7,5},{8,10},{9,11},{10,... | collective-permute-start | bytes 393224 | tf_op jit(solution)/shard_map/ppermute | solution.py:35
  8.2 0.0 collective-permute-start.3
  8.3 5.7 %collective-permute-done.refs_1_ = f32[256,128]{1,0:T(8,128)S(1)} collective-permute-done((f32[256,128]{1,0:T(8,128)}, f32[256,128]{1,0:T(8,128)S(1)}, u32[]{:S(2)}, u32[]{:S(2)}) %collective-permute-start) | collective-permute-done | bytes 131104 | tf_op jit(solution)/shard_map/ppermute | solution.py:35
  13.9 0.8 %collective-permute-start.2 = (f32[256,128]{1,0:T(8,128)}, f32[256,128]{1,0:T(8,128)S(1)}, u32[]{:S(2)}, u32[]{:S(2)}) collective-permute-start(f32[256,128]{1,0:T(8,128)} %refs_3_.2), channel_id=1, source_target_pairs={{0,1},{1,0},{2,3},{3,2},{4,5},{5,4},{6,7},{7,6},{8,9},{9,8},{10,11... | collective-permute-start | bytes 393224 | tf_op jit(solution)/shard_map/ppermute | solution.py:35
  14.8 0.0 collective-permute-done.4.refs_4_
  14.8 0.0 collective-permute-start.5
  14.8 0.0 collective-permute-done.6.refs_6_
  14.8 0.5 collective-permute-start.7
  15.3 0.0 collective-permute-done.8.refs_8_
  15.3 0.1 collective-permute-start.9
  15.3 3.8 %collective-permute-done.2.refs_0_ = f32[256,128]{1,0:T(8,128)S(1)} collective-permute-done((f32[256,128]{1,0:T(8,128)}, f32[256,128]{1,0:T(8,128)S(1)}, u32[]{:S(2)}, u32[]{:S(2)}) %collective-permute-start.2) | collective-permute-done | bytes 131104 | tf_op jit(solution)/shard_map/ppermute | solution.py:35
  19.1 0.8 %collective-permute-start.1 = (f32[256,128]{1,0:T(8,128)S(1)}, f32[256,128]{1,0:T(8,128)S(1)}, u32[]{:S(2)}, u32[]{:S(2)}) collective-permute-start(f32[256,128]{1,0:T(8,128)S(1)} %collective-permute-done.refs_1_), channel_id=1, source_target_pairs={{0,1},{1,0},{2,3},{3,2},{4,5},{5,4},{6,7},{7,6},{8,9},{9,8},{10,11... | collective-permute-start | bytes 393224 | tf_op jit(solution)/shard_map/ppermute | solution.py:35
  19.9 0.0 collective-permute-done.3.refs_3_
  19.9 3.3 %collective-permute-start.12 = (f32[96,512]{1,0:T(8,128)}, f32[96,512]{1,0:T(8,128)S(1)}, u32[]{:S(2)}, u32[]{:S(2)}) collective-permute-start(f32[96,512]{1,0:T(8,128)} %refs_4_.2), channel_id=1, source_target_pairs={{0,2},{1,3},{2,0},{3,1},{4,6},{5,7},{6,4},{7,5},{8,10},{9,11},{10,... | collective-permute-start | bytes 589832 | tf_op jit(solution)/shard_map/ppermute | solution.py:35
  23.2 1.7 %shard_map.104 = (s32[8]{0:T(128)S(1)}, f32[4,1,128]{2,1,0:T(1,128)S(1)}, f32[256,128]{1,0:T(8,128)S(1)}, bf16[96,512]{1,0:T(8,128)(2,1)S(1)}, bf16[96,512]{1,0:T(8,128)(2,1)S(1)}) custom-call(s32[4,8]{1,0:T(4,128)} %refs_0_.3, s32[4,8]{1,0:T(4,128)} %refs_1_.2, f32[4,1,128]{2,1,0:T(1,128)} %bitcast.1, f32[256,128]{1,0:T(8,128)} %refs_3_.2, f32[96,512]{1,0:T(8,128)} %refs_4_.2), custom_call_target="tpu_custom_call" | custom-call | bytes 2097152 | tf_op jit(solution)/shard_map/pallas_call | solution.py:270
  25.0 0.0 collective-permute-done.5.refs_5_
  25.0 0.0 collective-permute-done.7.refs_7_
  25.0 0.0 collective-permute-done.9.refs_9_
  25.0 1.7 %shard_map.106 = (bf16[256,512]{1,0:T(8,128)(2,1)S(1)}, bf16[256,512]{1,0:T(8,128)(2,1)S(1)}, f32[3,256,256]{2,1,0:T(8,128)S(1)}, bf16[3,256,128]{2,1,0:T(8,128)(2,1)S(1)}, bf16[3,256,128]{2,1,0:T(8,128)(2,1)S(1)}) custom-call(s32[8]{0:T(128)S(1)} %get-tuple-element.24.slots_ref.refs_0_, f32[4,1,128]{2,1,0:T(1,128)S(1)} %get-tuple-element.29.occ_ref, ...), custom_call_target="tpu_custom_call" | custom-call | flops 603979776 | bytes 2097152 | tf_op jit(solution)/shard_map/pallas_call | solution.py:296
  26.7 0.0 collective-permute-done.1.row_ref
  26.7 0.5 shard_map.107
  27.2 1.8 %collective-permute-start.10 = (f32[256,256]{1,0:T(8,128)S(1)}, f32[256,256]{1,0:T(8,128)S(1)}, u32[]{:S(2)}, u32[]{:S(2)}) collective-permute-start(f32[256,256]{1,0:T(8,128)S(1)} %get-tuple-element.42), channel_id=1, source_target_pairs={{0,3},{1,2},{2,1},{3,0},{4,7},{5,6},{6,5},{7,4},{8,11},{9,10},{10,... | collective-permute-start | bytes 786440 | tf_op jit(solution)/shard_map/ppermute | solution.py:35
  28.9 8.8 %collective-permute-done.12.refs_8_ = f32[96,512]{1,0:T(8,128)S(1)} collective-permute-done((f32[96,512]{1,0:T(8,128)}, f32[96,512]{1,0:T(8,128)S(1)}, u32[]{:S(2)}, u32[]{:S(2)}) %collective-permute-start.12) | collective-permute-done | bytes 196640 | tf_op jit(solution)/shard_map/ppermute | solution.py:35
  37.8 1.5 %collective-permute-start.14 = (f32[96,512]{1,0:T(8,128)S(1)}, f32[96,512]{1,0:T(8,128)S(1)}, u32[]{:S(2)}, u32[]{:S(2)}) collective-permute-start(f32[96,512]{1,0:T(8,128)S(1)} %collective-permute-done.12.refs_8_), channel_id=1, source_target_pairs={{0,8},{4,12},{8,0},{12,4},{16,24},{20,28},{24,16},{28,20},{1,9},{5... | collective-permute-start | bytes 589832 | tf_op jit(solution)/shard_map/ppermute | solution.py:35
  39.3 1.5 %collective-permute-start.16 = (f32[96,512]{1,0:T(8,128)S(1)}, f32[96,512]{1,0:T(8,128)S(1)}, u32[]{:S(2)}, u32[]{:S(2)}) collective-permute-start(f32[96,512]{1,0:T(8,128)S(1)} %collective-permute-done.12.refs_8_), channel_id=1, source_target_pairs={{0,16},{4,20},{8,24},{12,28},{16,0},{20,4},{24,8},{28,12},{1,17},{... | collective-permute-start | bytes 589832 | tf_op jit(solution)/shard_map/ppermute | solution.py:35
  40.8 0.5 collective-permute-start.18
  41.3 0.2 collective-permute-start.11
  41.5 2.0 %collective-permute-done.14.refs_10_ = f32[96,512]{1,0:T(8,128)S(1)} collective-permute-done((f32[96,512]{1,0:T(8,128)S(1)}, f32[96,512]{1,0:T(8,128)S(1)}, u32[]{:S(2)}, u32[]{:S(2)}) %collective-permute-start.14) | collective-permute-done | bytes 196640 | tf_op jit(solution)/shard_map/ppermute | solution.py:35
  43.5 0.0 collective-permute-start.13
  43.5 2.7 %collective-permute-done.16.refs_12_ = f32[96,512]{1,0:T(8,128)S(1)} collective-permute-done((f32[96,512]{1,0:T(8,128)S(1)}, f32[96,512]{1,0:T(8,128)S(1)}, u32[]{:S(2)}, u32[]{:S(2)}) %collective-permute-start.16) | collective-permute-done | bytes 196640 | tf_op jit(solution)/shard_map/ppermute | solution.py:35
  46.1 0.0 collective-permute-start.15
  46.1 1.2 %collective-permute-done.18.refs_14_ = f32[96,512]{1,0:T(8,128)S(1)} collective-permute-done((f32[96,512]{1,0:T(8,128)S(1)}, f32[96,512]{1,0:T(8,128)S(1)}, u32[]{:S(2)}, u32[]{:S(2)}) %collective-permute-start.18) | collective-permute-done | bytes 196640 | tf_op jit(solution)/shard_map/ppermute | solution.py:35
  47.4 0.0 collective-permute-start.17
  47.4 0.0 collective-permute-done.10.refs_0_
  47.4 0.5 collective-permute-start.19
  47.9 1.6 %shard_map.105 = (bf16[4,256,256]{2,1,0:T(8,128)(2,1)S(1)}, bf16[4,256,256]{2,1,0:T(8,128)(2,1)S(1)}, f32[256,128]{1,0:T(8,128)S(1)}, f32[1,256,256]{2,1,0:T(8,128)S(1)}) custom-call(s32[4,8]{1,0:T(4,128)} %refs_0_.3, s32[4,8]{1,0:T(4,128)} %refs_1_.3, f32[1,256,1024]{2,1,0:T(8,128)} %refs_2_.1, f32[1,256]{1,0:T(1,128)} %refs_3_.3, f32[1,256,256]{2,1,0:T(8,128)} %refs_4_.3), custom_call_target="tpu_custom_call" | custom-call | bytes 2097152 | tf_op jit(solution)/shard_map/pallas_call | solution.py:262
  49.4 0.4 shard_map.108
  49.8 0.0 collective-permute-done.11.refs_1_
  49.8 0.4 shard_map.109.refs_5_
  50.3 0.0 collective-permute-done.13.refs_9_
  50.3 0.0 collective-permute-done.15.refs_11_
  50.3 0.0 collective-permute-done.17.refs_13_
  50.3 0.0 collective-permute-done.19.refs_15_
  50.3 2.2 %shard_map.110 = (f32[1,256]{1,0:T(1,128)}, f32[1,256]{1,0:T(1,128)}) custom-call(s32[8]{0:T(128)S(1)} %get-tuple-element.24.slots_ref.refs_0_, bf16[4,256,256]{2,1,0:T(8,128)(2,1)S(1)} %get-tuple-element.25.phi_hi.refs_1_, bf16[4,256,256]{2,1,0:T(8,128)(2,1)S(1)} %get-tuple-element.26.phi_lo.refs_2_, f32[1,256,256]{2,1,0:T(8,128)S(1)} %get-tuple-element.27.refs_3_, ...), custom_call_target="tpu_custom_call" | custom-call | bytes 2097152 | tf_op jit(solution)/shard_map/pallas_call | solution.py:334
Async XLA Ops:
  0.6 14.1 %collective-permute-start.4 = (f32[96,512]{1,0:T(8,128)}, f32[96,512]{1,0:T(8,128)S(1)}, u32[]{:S(2)}, u32[]{:S(2)}) collective-permute-start(f32[96,512]{1,0:T(8,128)} %refs_4_.2), channel_id=1, source_target_pairs={{0,8},{4,12},{8,0},{12,4},{16,24},{20,28},{24,16},{28,20},{1,9},{5... | collective-permute-start | bytes 589832 | tf_op jit(solution)/shard_map/ppermute | solution.py:35
  3.7 11.1 %collective-permute-start.6 = (f32[96,512]{1,0:T(8,128)}, f32[96,512]{1,0:T(8,128)S(1)}, u32[]{:S(2)}, u32[]{:S(2)}) collective-permute-start(f32[96,512]{1,0:T(8,128)} %refs_4_.2), channel_id=1, source_target_pairs={{0,16},{4,20},{8,24},{12,28},{16,0},{20,4},{24,8},{28,12},{1,17},{... | collective-permute-start | bytes 589832 | tf_op jit(solution)/shard_map/ppermute | solution.py:35
  5.2 10.1 %collective-permute-start.8 = (f32[96,512]{1,0:T(8,128)}, f32[96,512]{1,0:T(8,128)S(1)}, u32[]{:S(2)}, u32[]{:S(2)}) collective-permute-start(f32[96,512]{1,0:T(8,128)} %refs_4_.2), channel_id=1, source_target_pairs={{0,24},{4,28},{8,16},{12,20},{16,8},{20,12},{24,0},{28,4},{1,25},{... | collective-permute-start | bytes 589832 | tf_op jit(solution)/shard_map/ppermute | solution.py:35
  5.2 8.7 %collective-permute-start = (f32[256,128]{1,0:T(8,128)}, f32[256,128]{1,0:T(8,128)S(1)}, u32[]{:S(2)}, u32[]{:S(2)}) collective-permute-start(f32[256,128]{1,0:T(8,128)} %refs_3_.2), channel_id=1, source_target_pairs={{0,2},{1,3},{2,0},{3,1},{4,6},{5,7},{6,4},{7,5},{8,10},{9,11},{10,... | collective-permute-start | bytes 393224 | tf_op jit(solution)/shard_map/ppermute | solution.py:35
  8.2 11.7 %collective-permute-start.3 = (f32[96,512]{1,0:T(8,128)}, f32[96,512]{1,0:T(8,128)S(1)}, u32[]{:S(2)}, u32[]{:S(2)}) collective-permute-start(f32[96,512]{1,0:T(8,128)} %refs_4_.2), channel_id=1, source_target_pairs={{0,4},{4,0},{8,12},{12,8},{16,20},{20,16},{24,28},{28,24},{1,5},{5... | collective-permute-start | bytes 589832 | tf_op jit(solution)/shard_map/ppermute | solution.py:35
  13.9 5.2 %collective-permute-start.2 = (f32[256,128]{1,0:T(8,128)}, f32[256,128]{1,0:T(8,128)S(1)}, u32[]{:S(2)}, u32[]{:S(2)}) collective-permute-start(f32[256,128]{1,0:T(8,128)} %refs_3_.2), channel_id=1, source_target_pairs={{0,1},{1,0},{2,3},{3,2},{4,5},{5,4},{6,7},{7,6},{8,9},{9,8},{10,11... | collective-permute-start | bytes 393224 | tf_op jit(solution)/shard_map/ppermute | solution.py:35
  14.8 10.2 %collective-permute-start.5 = (f32[96,512]{1,0:T(8,128)S(1)}, f32[96,512]{1,0:T(8,128)S(1)}, u32[]{:S(2)}, u32[]{:S(2)}) collective-permute-start(f32[96,512]{1,0:T(8,128)S(1)} %collective-permute-done.4.refs_4_), channel_id=1, source_target_pairs={{0,4},{4,0},{8,12},{12,8},{16,20},{20,16},{24,28},{28,24},{1,5},{5... | collective-permute-start | bytes 589832 | tf_op jit(solution)/shard_map/ppermute | solution.py:35
  14.8 10.2 %collective-permute-start.7 = (f32[96,512]{1,0:T(8,128)S(1)}, f32[96,512]{1,0:T(8,128)S(1)}, u32[]{:S(2)}, u32[]{:S(2)}) collective-permute-start(f32[96,512]{1,0:T(8,128)S(1)} %collective-permute-done.6.refs_6_), channel_id=1, source_target_pairs={{0,4},{4,0},{8,12},{12,8},{16,20},{20,16},{24,28},{28,24},{1,5},{5... | collective-permute-start | bytes 589832 | tf_op jit(solution)/shard_map/ppermute | solution.py:35
  15.3 9.7 %collective-permute-start.9 = (f32[96,512]{1,0:T(8,128)S(1)}, f32[96,512]{1,0:T(8,128)S(1)}, u32[]{:S(2)}, u32[]{:S(2)}) collective-permute-start(f32[96,512]{1,0:T(8,128)S(1)} %collective-permute-done.8.refs_8_), channel_id=1, source_target_pairs={{0,4},{4,0},{8,12},{12,8},{16,20},{20,16},{24,28},{28,24},{1,5},{5... | collective-permute-start | bytes 589832 | tf_op jit(solution)/shard_map/ppermute | solution.py:35
  19.1 7.5 %collective-permute-start.1 = (f32[256,128]{1,0:T(8,128)S(1)}, f32[256,128]{1,0:T(8,128)S(1)}, u32[]{:S(2)}, u32[]{:S(2)}) collective-permute-start(f32[256,128]{1,0:T(8,128)S(1)} %collective-permute-done.refs_1_), channel_id=1, source_target_pairs={{0,1},{1,0},{2,3},{3,2},{4,5},{5,4},{6,7},{7,6},{8,9},{9,8},{10,11... | collective-permute-start | bytes 393224 | tf_op jit(solution)/shard_map/ppermute | solution.py:35
  19.9 17.8 %collective-permute-start.12 = (f32[96,512]{1,0:T(8,128)}, f32[96,512]{1,0:T(8,128)S(1)}, u32[]{:S(2)}, u32[]{:S(2)}) collective-permute-start(f32[96,512]{1,0:T(8,128)} %refs_4_.2), channel_id=1, source_target_pairs={{0,2},{1,3},{2,0},{3,1},{4,6},{5,7},{6,4},{7,5},{8,10},{9,11},{10,... | collective-permute-start | bytes 589832 | tf_op jit(solution)/shard_map/ppermute | solution.py:35
  27.2 20.2 %collective-permute-start.10 = (f32[256,256]{1,0:T(8,128)S(1)}, f32[256,256]{1,0:T(8,128)S(1)}, u32[]{:S(2)}, u32[]{:S(2)}) collective-permute-start(f32[256,256]{1,0:T(8,128)S(1)} %get-tuple-element.42), channel_id=1, source_target_pairs={{0,3},{1,2},{2,1},{3,0},{4,7},{5,6},{6,5},{7,4},{8,11},{9,10},{10,... | collective-permute-start | bytes 786440 | tf_op jit(solution)/shard_map/ppermute | solution.py:35
  37.8 5.7 %collective-permute-start.14 = (f32[96,512]{1,0:T(8,128)S(1)}, f32[96,512]{1,0:T(8,128)S(1)}, u32[]{:S(2)}, u32[]{:S(2)}) collective-permute-start(f32[96,512]{1,0:T(8,128)S(1)} %collective-permute-done.12.refs_8_), channel_id=1, source_target_pairs={{0,8},{4,12},{8,0},{12,4},{16,24},{20,28},{24,16},{28,20},{1,9},{5... | collective-permute-start | bytes 589832 | tf_op jit(solution)/shard_map/ppermute | solution.py:35
  39.3 6.8 %collective-permute-start.16 = (f32[96,512]{1,0:T(8,128)S(1)}, f32[96,512]{1,0:T(8,128)S(1)}, u32[]{:S(2)}, u32[]{:S(2)}) collective-permute-start(f32[96,512]{1,0:T(8,128)S(1)} %collective-permute-done.12.refs_8_), channel_id=1, source_target_pairs={{0,16},{4,20},{8,24},{12,28},{16,0},{20,4},{24,8},{28,12},{1,17},{... | collective-permute-start | bytes 589832 | tf_op jit(solution)/shard_map/ppermute | solution.py:35
  40.8 6.6 %collective-permute-start.18 = (f32[96,512]{1,0:T(8,128)S(1)}, f32[96,512]{1,0:T(8,128)S(1)}, u32[]{:S(2)}, u32[]{:S(2)}) collective-permute-start(f32[96,512]{1,0:T(8,128)S(1)} %collective-permute-done.12.refs_8_), channel_id=1, source_target_pairs={{0,24},{4,28},{8,16},{12,20},{16,8},{20,12},{24,0},{28,4},{1,25},{... | collective-permute-start | bytes 589832 | tf_op jit(solution)/shard_map/ppermute | solution.py:35
  41.3 8.6 %collective-permute-start.11 = (f32[256,256]{1,0:T(8,128)S(1)}, f32[256,256]{1,0:T(8,128)S(1)}, u32[]{:S(2)}, u32[]{:S(2)}) collective-permute-start(f32[256,256]{1,0:T(8,128)S(1)} %get-tuple-element.43), channel_id=1, source_target_pairs={{0,1},{1,0},{2,3},{3,2},{4,5},{5,4},{6,7},{7,6},{8,9},{9,8},{10,11... | collective-permute-start | bytes 786440 | tf_op jit(solution)/shard_map/ppermute | solution.py:35
  43.5 6.8 %collective-permute-start.13 = (f32[96,512]{1,0:T(8,128)S(1)}, f32[96,512]{1,0:T(8,128)S(1)}, u32[]{:S(2)}, u32[]{:S(2)}) collective-permute-start(f32[96,512]{1,0:T(8,128)S(1)} %collective-permute-done.12.refs_8_), channel_id=1, source_target_pairs={{0,4},{4,0},{8,12},{12,8},{16,20},{20,16},{24,28},{28,24},{1,5},{5... | collective-permute-start | bytes 589832 | tf_op jit(solution)/shard_map/ppermute | solution.py:35
  46.1 4.2 %collective-permute-start.15 = (f32[96,512]{1,0:T(8,128)S(1)}, f32[96,512]{1,0:T(8,128)S(1)}, u32[]{:S(2)}, u32[]{:S(2)}) collective-permute-start(f32[96,512]{1,0:T(8,128)S(1)} %collective-permute-done.14.refs_10_), channel_id=1, source_target_pairs={{0,4},{4,0},{8,12},{12,8},{16,20},{20,16},{24,28},{28,24},{1,5},{5... | collective-permute-start | bytes 589832 | tf_op jit(solution)/shard_map/ppermute | solution.py:35
  47.4 2.9 %collective-permute-start.17 = (f32[96,512]{1,0:T(8,128)S(1)}, f32[96,512]{1,0:T(8,128)S(1)}, u32[]{:S(2)}, u32[]{:S(2)}) collective-permute-start(f32[96,512]{1,0:T(8,128)S(1)} %collective-permute-done.16.refs_12_), channel_id=1, source_target_pairs={{0,4},{4,0},{8,12},{12,8},{16,20},{20,16},{24,28},{28,24},{1,5},{5... | collective-permute-start | bytes 589832 | tf_op jit(solution)/shard_map/ppermute | solution.py:35
  47.4 2.9 %collective-permute-start.19 = (f32[96,512]{1,0:T(8,128)S(1)}, f32[96,512]{1,0:T(8,128)S(1)}, u32[]{:S(2)}, u32[]{:S(2)}) collective-permute-start(f32[96,512]{1,0:T(8,128)S(1)} %collective-permute-done.18.refs_14_), channel_id=1, source_target_pairs={{0,4},{4,0},{8,12},{12,8},{16,20},{20,16},{24,28},{28,24},{1,5},{5... | collective-permute-start | bytes 589832 | tf_op jit(solution)/shard_map/ppermute | solution.py:35

commit v3 on v2

--- a/solution.py
+++ b/solution.py
@@ -56,11 +56,19 @@
     return [pieces[k] for k in range(8)]
 
 
-def place(row, k, pieces):
-    size = pieces[k].shape[0]
-    if len(pieces) == 1:
-        return pl.ds(0, size)
-    return pl.ds(pl.multiple_of((row ^ k) * size, 16), size)
+FIRST = (0, 1, 2, 4, 6)
+
+
+def fill(row, count, ks, refs, high, low):
+    for k, ref in zip(ks, refs):
+        size = ref.shape[0]
+        at = pl.ds(pl.multiple_of((row ^ k) * size, 16), size) if count > 1 else pl.ds(0, size)
+        high[at, :], low[at, :] = split(ref[...])
+
+
+def two(count):
+    first = [k for k in FIRST if k < count]
+    return first, [k for k in range(count) if k not in first]
 
 
 def requests(owner_ref, values_ref, batch, holder):
@@ -117,8 +125,8 @@
 
 def tables_kernel(served, far, *refs):
     sources, refs = refs[:5], refs[5:]
-    slots_ref, occ_ref, own_row, own_hi, own_lo = refs[:5]
-    row_ref, chunk_ref, owner_ref, slot_ref, sems = refs[5:]
+    slots_ref, occ_ref, own_row, chunk_ref = refs[:4]
+    row_ref, owner_ref, slot_ref, sems = refs[4:]
     targets = owner_ref, slot_ref, occ_ref, row_ref, chunk_ref
     for copy in start_copies(sources, targets, sems):
         copy.wait()
@@ -130,28 +138,32 @@
     slots, _ = requests(owner_ref, slot_ref, col, col ^ far)
     for j in range(PAIR):
         slots_ref[len(served) * PAIR + j] = slots[j]
-    own_hi[...], own_lo[...] = split(chunk_ref[...])
     own_row[...] = row_ref[...] * occ_ref[col]
 
 
-def early_kernel(groups, n_served, n_chunks, slots_ref, occ_ref, own_row, own_hi, own_lo, *refs):
+def split_kernel(groups, count, occ_ref, own_row, *refs):
     row_refs, refs = refs[: groups - 2], refs[groups - 2 :]
-    chunk_refs, refs = refs[:n_chunks], refs[n_chunks:]
-    left_hi, left_lo, partial_ref, last_hi, last_lo, scaled_ref, col_hi, col_lo = refs
-    row, col = lax.axis_index("row"), lax.axis_index("col")
-    last = col ^ (groups - 1)
-    for k in range(n_chunks):
-        at = place(row, k, chunk_refs)
-        if k == 0 and n_chunks > 1:
-            col_hi[at, :], col_lo[at, :] = own_hi[...], own_lo[...]
-        else:
-            col_hi[at, :], col_lo[at, :] = split(chunk_refs[k][...])
+    first, _ = two(count)
+    chunk_refs, refs = refs[: len(first)], refs[len(first) :]
+    left_hi, left_lo, col_hi, col_lo, scaled_ref = refs
+    col = lax.axis_index("col")
+    fill(lax.axis_index("row"), count, first, chunk_refs, col_hi, col_lo)
     scaled_ref[col] = own_row[...]
     for k in range(1, groups - 1):
         scaled_ref[col ^ k] = row_refs[k - 1][...] * occ_ref[col ^ k]
-    scaled_ref[last] = jnp.zeros_like(own_row)
-    left = split(jnp.concatenate([scaled_ref[k] for k in range(groups)], axis=1))
-    left_hi[...], left_lo[...] = left
+    scaled_ref[col ^ (groups - 1)] = jnp.zeros_like(own_row)
+    left_hi[...], left_lo[...] = split(
+        jnp.concatenate([scaled_ref[k] for k in range(groups)], axis=1)
+    )
+
+
+def early_kernel(groups, n_served, count, slots_ref, left_hi, left_lo, *refs):
+    _, rest = two(count)
+    chunk_refs, refs = refs[2 : 2 + len(rest)], refs[2 + len(rest) :]
+    col_hi, col_lo, partial_ref, last_hi, last_lo = refs
+    fill(lax.axis_index("row"), count, rest, chunk_refs, col_hi, col_lo)
+    last = lax.axis_index("col") ^ (groups - 1)
+    left = left_hi[...], left_lo[...]
     quarter = last_hi.shape[2]
     for i in range(n_served):
         right = tiles((col_hi, col_lo), slots_ref, i)
@@ -190,21 +202,24 @@
         )
 
 
-def strips_kernel(others, phi_hi, phi_lo, own_ref, *refs):
+def strips_kernel(others, count, phi_hi, phi_lo, own_ref, *refs):
+    strips, refs = refs[: len(others)], refs[len(others) :]
+    first, _ = two(count)
+    chunk_refs, (out_ref, col_hi, col_lo) = refs[: len(first)], refs[len(first) :]
     total = own_ref[...]
-    for k, strip_ref in zip(others, refs):
+    for k, strip_ref in zip(others, strips):
         total += dot3((phi_hi[k], phi_lo[k]), split(strip_ref[...]))
-    refs[-1][...] = total
-
-
-def final_kernel(far, index, n_chunks, *refs):
-    slots_ref, phi_hi, phi_lo, rows_ref, pot_ref, sum_ref, left_hi, left_lo = refs[:8]
-    chunks, (density_ref, potential_ref, block_ref) = refs[8 : 8 + n_chunks], refs[8 + n_chunks :]
-    row = lax.axis_index("row")
-    for k in range(n_chunks):
-        block_ref[place(row, k, chunks), :] = chunks[k][...]
-    columns = tiles((block_ref,), slots_ref, index)[0]
-    strip = dot3((left_hi[...], left_lo[...]), split(columns))
+    out_ref[...] = total
+    fill(lax.axis_index("row"), count, first, chunk_refs, col_hi, col_lo)
+
+
+def final_kernel(far, index, count, slots_ref, phi_hi, phi_lo, rows_ref, pot_ref, *refs):
+    sum_ref, left_hi, left_lo = refs[:3]
+    _, rest = two(count)
+    chunk_refs, refs = refs[5 : 5 + len(rest)], refs[5 + len(rest) :]
+    density_ref, potential_ref, col_hi, col_lo = refs
+    fill(lax.axis_index("row"), count, rest, chunk_refs, col_hi, col_lo)
+    strip = dot3((left_hi[...], left_lo[...]), tiles((col_hi, col_lo), slots_ref, index))
     coupled = sum_ref[...] + dot3((phi_hi[far], phi_lo[far]), split(strip))
     field = rows_ref[0] * coupled
     weights = pot_ref[...]
@@ -218,7 +233,7 @@
     )[:1]
 
 
-def call(kernel, in_specs, outs, scratch=(), flops=0):
+def call(kernel, in_specs, outs, scratch=(), flops=0, aliases={}):
     out_specs = [SMEM if len(o.shape) == 1 else VMEM for o in outs]
     return pl.pallas_call(
         kernel,
@@ -226,6 +241,7 @@
         in_specs=in_specs,
         out_specs=out_specs,
         scratch_shapes=list(scratch),
+        input_output_aliases=aliases,
         compiler_params=PARAMS,
         cost_estimate=pl.CostEstimate(flops=flops, bytes_accessed=2 << 20, transcendentals=0),
     )
@@ -267,18 +283,17 @@
         + [pltpu.VMEM(a.shape, jnp.float32) for a in (phi_col, potential)]
         + [pltpu.SemaphoreType.DMA((5,))],
     )(*in_hbm(tile_owner, correlation, phi_col, potential, phi_row))
-    slots, occ, own_row, own_hi, own_lo = call(
+    slots, occ, own_row, own_chunk = call(
         functools.partial(tables_kernel, served, far),
         [HBM] * 5,
         [
             jax.ShapeDtypeStruct(((n_served + 1) * PAIR,), jnp.int32),
             f32(groups, 1, quarter),
             f32(rows, quarter),
-            *[bf16(*column_vectors.shape)] * 2,
+            f32(*column_vectors.shape),
         ],
         [
             pltpu.VMEM((rows, quarter), jnp.float32),
-            pltpu.VMEM(column_vectors.shape, jnp.float32),
             *tables,
             pltpu.SemaphoreType.DMA((5,)),
         ],
@@ -291,22 +306,25 @@
             column_vectors,
         )
     )
-    if len(chunks) > 1:
-        chunks[0] = own_hi
-    left_hi, left_lo, partial, right_hi, right_lo = call(
-        functools.partial(early_kernel, groups, n_served, len(chunks)),
-        [SMEM] + [VMEM] * (4 + groups - 2 + len(chunks)),
-        [
-            *[bf16(rows, states)] * 2,
-            f32(n_served, rows, width),
-            *[bf16(n_served, width, quarter)] * 2,
-        ],
-        [
-            pltpu.VMEM((groups, rows, quarter), jnp.float32),
-            *[pltpu.VMEM((block, states), jnp.bfloat16)] * 2,
-        ],
+    count = len(chunks)
+    first, rest = two(count)
+    if count > 1:
+        chunks[0] = own_chunk
+    halves = [bf16(block, states)] * 2
+    left_hi, left_lo, col_hi, col_lo = call(
+        functools.partial(split_kernel, groups, count),
+        [VMEM] * (groups + len(first)),
+        [bf16(rows, states)] * 2 + halves,
+        [pltpu.VMEM((groups, rows, quarter), jnp.float32)],
+    )(occ, own_row, *row_pieces[1:-1], *(chunks[k] for k in first))
+    _, _, partial, right_hi, right_lo = call(
+        functools.partial(early_kernel, groups, n_served, count),
+        [SMEM] + [VMEM] * (4 + len(rest)),
+        [*halves, f32(n_served, rows, width), *[bf16(n_served, width, quarter)] * 2],
+        (),
         6 * rows * width * states * n_served,
-    )(slots, occ, own_row, own_hi, own_lo, *row_pieces[1:-1], *chunks)
+        {3: 0, 4: 1},
+    )(slots, left_hi, left_lo, col_hi, col_lo, *(chunks[k] for k in rest))
     row_hi, row_lo, *strips = call(
         functools.partial(density_kernel, groups),
         [VMEM] * 5,
@@ -323,20 +341,25 @@
         (),
         6 * points * rows * width,
     )(phi_hi, phi_lo, strips[0], left_hi, left_lo, row_hi, row_lo)
-    summed = call(
-        functools.partial(strips_kernel, others),
-        [VMEM] * (3 + len(others)),
-        [f32(points, rows)],
+    summed, far_hi, far_lo = call(
+        functools.partial(strips_kernel, others, count),
+        [VMEM] * (3 + len(others) + len(first)),
+        [f32(points, rows), *halves],
         (),
         6 * points * rows * width * len(others),
-    )(phi_hi, phi_lo, own, *arrived)[0]
+    )(phi_hi, phi_lo, own, *arrived, *(far_chunks[k] for k in first))
     return tuple(
         call(
-            functools.partial(final_kernel, far, n_served, len(far_chunks)),
-            [SMEM] + [VMEM] * (7 + len(far_chunks)),
-            [f32(1, points), f32(1, rows)],
-            [pltpu.VMEM((block, states), jnp.float32)],
-        )(slots, phi_hi, phi_lo, rows_field, pot, summed, full_hi, full_lo, *far_chunks)
+            functools.partial(final_kernel, far, n_served, count),
+            [SMEM] + [VMEM] * (9 + len(rest)),
+            [f32(1, points), f32(1, rows), *halves],
+            (),
+            0,
+            {8: 2, 9: 3},
+        )(
+            *(slots, phi_hi, phi_lo, rows_field, pot, summed, full_hi, full_lo, far_hi, far_lo),
+            *(far_chunks[k] for k in rest),
+        )[:2]
     )
 
 

time: 52.8 us -> 49.6 us (0.939)
  waiting for transfers between devices: 24.2 us -> 21.9 us
  starting transfers between devices: 19.1 us -> 18 us
    ppermute x20, waiting for transfers between devices: 24.2 us -> 21.9 us  [flip(): return lax.ppermute(x, axis, [(i, i ^ bit) for i in range(size)])]
    ppermute x20, starting transfers between devices: 19.1 us -> 18 us  [flip(): return lax.ppermute(x, axis, [(i, i ^ bit) for i in range(size)])]
    pallas_call x3 -> x4, Pallas kernels: 4.33 us -> 4.58 us  [the longest x1 2.19 us: per_device(): call(functools.partial(final_kernel, far, n_served, count), [SMEM] + [VME...]
  transfers between devices with their start and end apart: 20 -> 20, of which waited for: 6 -> 7; matrix products, arithmetic and copies ran while one was open for 0% -> 0% of each run, Pallas kernels for 12% -> 13%
where the time goes in v3:
time: 49.6 us; the launch traced here: 49.4 us
  waiting for transfers between devices  21.9 us (44%)
  starting transfers between devices  18 us (36%)
  Pallas kernels  8.74 us (18%)
  between operations  0.73 us (1%)
    ppermute x20, waiting for transfers between devices, flip(): return lax.ppermute(x, axis, [(i, i ^ bit) for i in range(size)])  21.9 us
    ppermute x20, starting transfers between devices, flip(): return lax.ppermute(x, axis, [(i, i ^ bit) for i in range(size)])  18 us
    pallas_call x1, Pallas kernels, per_device(): call(functools.partial(final_kernel, far, n_served, count), [SMEM] + [VME...  2.19 us
    pallas_call x1, Pallas kernels, per_device(): call(functools.partial(tables_kernel, served, far), [HBM] * 5, [jax.Shape...  1.75 us
    pallas_call x1, Pallas kernels, per_device(): call(basis_kernel, [HBM] * 5, [bf16(groups, points, width)] * 2 + [f32(po...  1.55 us
    pallas_call x1, Pallas kernels, per_device(): call(functools.partial(early_kernel, groups, n_served, count), [SMEM] + [...  1.47 us
  transfers between devices with their start and end apart: 20, of which 7 were waited for; matrix products, arithmetic and copies ran while one was open for 0% of the time, Pallas kernels for 13%

profile of v3, /device:TPU:0, one launch (start us, length us, event | category | flops | bytes accessed | tf_op | source)
XLA Modules:
  0.0 49.4 jit_solution(7204233631390965667)
XLA Ops:
  0.6 4.1 %collective-permute-start = (f32[256,128]{1,0:T(8,128)}, f32[256,128]{1,0:T(8,128)S(1)}, u32[]{:S(2)}, u32[]{:S(2)}) collective-permute-start(f32[256,128]{1,0:T(8,128)} %refs_3_.2), channel_id=1, source_target_pairs={{0,2},{1,3},{2,0},{3,1},{4,6},{5,7},{6,4},{7,5},{8,10},{9,11},{10,... | collective-permute-start | bytes 393224 | tf_op jit(solution)/shard_map/ppermute | solution.py:35
  4.8 1.5 %collective-permute-start.4 = (f32[96,512]{1,0:T(8,128)}, f32[96,512]{1,0:T(8,128)S(1)}, u32[]{:S(2)}, u32[]{:S(2)}) collective-permute-start(f32[96,512]{1,0:T(8,128)} %refs_4_.2), channel_id=1, source_target_pairs={{0,8},{4,12},{8,0},{12,4},{16,24},{20,28},{24,16},{28,20},{1,9},{5... | collective-permute-start | bytes 589832 | tf_op jit(solution)/shard_map/ppermute | solution.py:35
  6.3 1.5 %collective-permute-start.5 = (f32[96,512]{1,0:T(8,128)}, f32[96,512]{1,0:T(8,128)S(1)}, u32[]{:S(2)}, u32[]{:S(2)}) collective-permute-start(f32[96,512]{1,0:T(8,128)} %refs_4_.2), channel_id=1, source_target_pairs={{0,16},{4,20},{8,24},{12,28},{16,0},{20,4},{24,8},{28,12},{1,17},{... | collective-permute-start | bytes 589832 | tf_op jit(solution)/shard_map/ppermute | solution.py:35
  7.8 0.5 collective-permute-start.6
  8.2 1.6 %collective-permute-start.2 = (f32[256,128]{1,0:T(8,128)}, f32[256,128]{1,0:T(8,128)S(1)}, u32[]{:S(2)}, u32[]{:S(2)}) collective-permute-start(f32[256,128]{1,0:T(8,128)} %refs_3_.2), channel_id=1, source_target_pairs={{0,1},{1,0},{2,3},{3,2},{4,5},{5,4},{6,7},{7,6},{8,9},{9,8},{10,11... | collective-permute-start | bytes 393224 | tf_op jit(solution)/shard_map/ppermute | solution.py:35
  9.8 1.5 %collective-permute-done.refs_1_ = f32[256,128]{1,0:T(8,128)S(1)} collective-permute-done((f32[256,128]{1,0:T(8,128)}, f32[256,128]{1,0:T(8,128)S(1)}, u32[]{:S(2)}, u32[]{:S(2)}) %collective-permute-start) | collective-permute-done | bytes 131104 | tf_op jit(solution)/shard_map/ppermute | solution.py:35
  11.4 0.0 collective-permute-start.12
  11.4 2.7 %collective-permute-done.2.refs_0_ = f32[256,128]{1,0:T(8,128)S(1)} collective-permute-done((f32[256,128]{1,0:T(8,128)}, f32[256,128]{1,0:T(8,128)S(1)}, u32[]{:S(2)}, u32[]{:S(2)}) %collective-permute-start.2) | collective-permute-done | bytes 131104 | tf_op jit(solution)/shard_map/ppermute | solution.py:35
  14.1 0.0 collective-permute-start.3
  14.1 0.0 collective-permute-done.4.refs_4_
  14.1 0.5 %collective-permute-start.7 = (f32[96,512]{1,0:T(8,128)S(1)}, f32[96,512]{1,0:T(8,128)S(1)}, u32[]{:S(2)}, u32[]{:S(2)}) collective-permute-start(f32[96,512]{1,0:T(8,128)S(1)} %collective-permute-done.4.refs_4_), channel_id=1, source_target_pairs={{0,4},{4,0},{8,12},{12,8},{16,20},{20,16},{24,28},{28,24},{1,5},{5... | collective-permute-start | bytes 589832 | tf_op jit(solution)/shard_map/ppermute | solution.py:35
  14.6 2.2 %collective-permute-done.5.refs_5_ = f32[96,512]{1,0:T(8,128)S(1)} collective-permute-done((f32[96,512]{1,0:T(8,128)}, f32[96,512]{1,0:T(8,128)S(1)}, u32[]{:S(2)}, u32[]{:S(2)}) %collective-permute-start.5) | collective-permute-done | bytes 196640 | tf_op jit(solution)/shard_map/ppermute | solution.py:35
  16.8 0.0 collective-permute-start.8
  16.8 0.0 collective-permute-done.6.refs_6_
  16.8 0.5 %collective-permute-start.9 = (f32[96,512]{1,0:T(8,128)S(1)}, f32[96,512]{1,0:T(8,128)S(1)}, u32[]{:S(2)}, u32[]{:S(2)}) collective-permute-start(f32[96,512]{1,0:T(8,128)S(1)} %collective-permute-done.6.refs_6_), channel_id=1, source_target_pairs={{0,4},{4,0},{8,12},{12,8},{16,20},{20,16},{24,28},{28,24},{1,5},{5... | collective-permute-start | bytes 589832 | tf_op jit(solution)/shard_map/ppermute | solution.py:35
  17.3 5.4 %collective-permute-done.12.refs_2_ = f32[96,512]{1,0:T(8,128)S(1)} collective-permute-done((f32[96,512]{1,0:T(8,128)}, f32[96,512]{1,0:T(8,128)S(1)}, u32[]{:S(2)}, u32[]{:S(2)}) %collective-permute-start.12) | collective-permute-done | bytes 196640 | tf_op jit(solution)/shard_map/ppermute | solution.py:35
  22.7 1.3 %collective-permute-start.14 = (f32[96,512]{1,0:T(8,128)S(1)}, f32[96,512]{1,0:T(8,128)S(1)}, u32[]{:S(2)}, u32[]{:S(2)}) collective-permute-start(f32[96,512]{1,0:T(8,128)S(1)} %collective-permute-done.12.refs_2_), channel_id=1, source_target_pairs={{0,8},{4,12},{8,0},{12,4},{16,24},{20,28},{24,16},{28,20},{1,9},{5... | collective-permute-start | bytes 589832 | tf_op jit(solution)/shard_map/ppermute | solution.py:35
  24.0 0.0 collective-permute-done.3.refs_3_
  24.0 0.0 collective-permute-start.1
  24.0 0.0 collective-permute-done.7.refs_2_
  24.0 1.6 %collective-permute-start.15 = (f32[96,512]{1,0:T(8,128)S(1)}, f32[96,512]{1,0:T(8,128)S(1)}, u32[]{:S(2)}, u32[]{:S(2)}) collective-permute-start(f32[96,512]{1,0:T(8,128)S(1)} %collective-permute-done.12.refs_2_), channel_id=1, source_target_pairs={{0,16},{4,20},{8,24},{12,28},{16,0},{20,4},{24,8},{28,12},{1,17},{... | collective-permute-start | bytes 589832 | tf_op jit(solution)/shard_map/ppermute | solution.py:35
  25.6 0.0 collective-permute-done.8.refs_3_
  25.6 0.6 %collective-permute-start.16 = (f32[96,512]{1,0:T(8,128)S(1)}, f32[96,512]{1,0:T(8,128)S(1)}, u32[]{:S(2)}, u32[]{:S(2)}) collective-permute-start(f32[96,512]{1,0:T(8,128)S(1)} %collective-permute-done.12.refs_2_), channel_id=1, source_target_pairs={{0,24},{4,28},{8,16},{12,20},{16,8},{20,12},{24,0},{28,4},{1,25},{... | collective-permute-start | bytes 589832 | tf_op jit(solution)/shard_map/ppermute | solution.py:35
  26.2 0.0 collective-permute-done.9.refs_4_
  26.2 0.0 collective-permute-start.13
  26.2 1.7 %shard_map.104 = (s32[8]{0:T(128)S(1)}, f32[4,1,128]{2,1,0:T(1,128)S(1)}, f32[256,128]{1,0:T(8,128)S(1)}, f32[96,512]{1,0:T(8,128)S(1)}) custom-call(s32[4,8]{1,0:T(4,128)} %refs_0_.3, s32[4,8]{1,0:T(4,128)} %refs_1_.2, f32[4,1,128]{2,1,0:T(1,128)} %bitcast.1, f32[256,128]{1,0:T(8,128)} %refs_3_.2, f32[96,512]{1,0:T(8,128)} %refs_4_.2), custom_call_target="tpu_custom_call" | custom-call | bytes 2097152 | tf_op jit(solution)/shard_map/pallas_call | solution.py:286
  28.0 0.4 shard_map.106
  28.4 1.5 %shard_map.107 = (bf16[768,512]{1,0:T(8,128)(2,1)S(1)}, bf16[768,512]{1,0:T(8,128)(2,1)S(1)}, f32[3,256,256]{2,1,0:T(8,128)S(1)}, bf16[3,256,128]{2,1,0:T(8,128)(2,1)S(1)}, bf16[3,256,128]{2,1,0:T(8,128)(2,1)S(1)}) custom-call(s32[8]{0:T(128)S(1)} %get-tuple-element.30.slots_ref, ...), custom_call_target="tpu_custom_call", output_to_operand_aliasing={{0}: (3, {}), {1}: (4, {})} | custom-call | flops 603979776 | bytes 2097152 | tf_op jit(solution)/shard_map/pallas_call | solution.py:320
  29.8 0.0 collective-permute-done.1.row_ref
  29.9 0.5 shard_map.108
  30.3 2.6 %collective-permute-start.10 = (f32[256,256]{1,0:T(8,128)S(1)}, f32[256,256]{1,0:T(8,128)S(1)}, u32[]{:S(2)}, u32[]{:S(2)}) collective-permute-start(f32[256,256]{1,0:T(8,128)S(1)} %get-tuple-element.49), channel_id=1, source_target_pairs={{0,3},{1,2},{2,1},{3,0},{4,7},{5,6},{6,5},{7,4},{8,11},{9,10},{10,... | collective-permute-start | bytes 786440 | tf_op jit(solution)/shard_map/ppermute | solution.py:35
  33.0 0.0 collective-permute-done.14.refs_4_
  33.0 1.1 %collective-permute-start.11 = (f32[256,256]{1,0:T(8,128)S(1)}, f32[256,256]{1,0:T(8,128)S(1)}, u32[]{:S(2)}, u32[]{:S(2)}) collective-permute-start(f32[256,256]{1,0:T(8,128)S(1)} %get-tuple-element.50), channel_id=1, source_target_pairs={{0,1},{1,0},{2,3},{3,2},{4,5},{5,4},{6,7},{7,6},{8,9},{9,8},{10,11... | collective-permute-start | bytes 786440 | tf_op jit(solution)/shard_map/ppermute | solution.py:35
  34.0 0.3 collective-permute-done.15.refs_5_
  34.3 0.0 collective-permute-start.17
  34.3 0.0 collective-permute-done.16.refs_6_
  34.3 0.5 %collective-permute-start.18 = (f32[96,512]{1,0:T(8,128)S(1)}, f32[96,512]{1,0:T(8,128)S(1)}, u32[]{:S(2)}, u32[]{:S(2)}) collective-permute-start(f32[96,512]{1,0:T(8,128)S(1)} %collective-permute-done.15.refs_5_), channel_id=1, source_target_pairs={{0,4},{4,0},{8,12},{12,8},{16,20},{20,16},{24,28},{28,24},{1,5},{5... | collective-permute-start | bytes 589832 | tf_op jit(solution)/shard_map/ppermute | solution.py:35
  34.8 0.0 collective-permute-done.13.refs_3_
  34.8 0.1 collective-permute-start.19
  34.9 1.6 %shard_map.105 = (bf16[4,256,256]{2,1,0:T(8,128)(2,1)S(1)}, bf16[4,256,256]{2,1,0:T(8,128)(2,1)S(1)}, f32[256,128]{1,0:T(8,128)S(1)}, f32[1,256,256]{2,1,0:T(8,128)S(1)}) custom-call(s32[4,8]{1,0:T(4,128)} %refs_0_.3, s32[4,8]{1,0:T(4,128)} %refs_1_.3, f32[1,256,1024]{2,1,0:T(8,128)} %refs_2_.1, f32[1,256]{1,0:T(1,128)} %refs_3_.3, f32[1,256,256]{2,1,0:T(8,128)} %refs_4_.3), custom_call_target="tpu_custom_call" | custom-call | bytes 2097152 | tf_op jit(solution)/shard_map/pallas_call | solution.py:278
  36.5 0.4 shard_map.109
  36.9 4.6 %collective-permute-done.10.refs_0_ = f32[256,256]{1,0:T(8,128)S(1)} collective-permute-done((f32[256,256]{1,0:T(8,128)S(1)}, f32[256,256]{1,0:T(8,128)S(1)}, u32[]{:S(2)}, u32[]{:S(2)}) %collective-permute-start.10) | collective-permute-done | bytes 262176 | tf_op jit(solution)/shard_map/ppermute | solution.py:35
  41.5 5.2 %collective-permute-done.11.refs_1_ = f32[256,256]{1,0:T(8,128)S(1)} collective-permute-done((f32[256,256]{1,0:T(8,128)S(1)}, f32[256,256]{1,0:T(8,128)S(1)}, u32[]{:S(2)}, u32[]{:S(2)}) %collective-permute-start.11) | collective-permute-done | bytes 262176 | tf_op jit(solution)/shard_map/ppermute | solution.py:35
  46.6 0.6 %shard_map.110 = (f32[256,256]{1,0:T(8,128)S(1)}, bf16[768,512]{1,0:T(8,128)(2,1)S(1)}, bf16[768,512]{1,0:T(8,128)(2,1)S(1)}) custom-call(bf16[4,256,256]{2,1,0:T(8,128)(2,1)S(1)} %get-tuple-element.31.phi_hi, bf16[4,256,256]{2,1,0:T(8,128)(2,1)S(1)} %get-tuple-element.32.phi_lo, f32[256,256]{1,0:T(8,128)S(1)} %get-tuple-element.48.own_ref, ...), custom_call_target="tpu_custom_call" | custom-call | flops 201326592 | bytes 2097152 | tf_op jit(solution)/shard_map/pallas_call | solution.py:344
  47.2 0.0 collective-permute-done.17.refs_5_
  47.2 0.0 collective-permute-done.18.refs_6_
  47.2 0.0 collective-permute-done.19.refs_7_
  47.2 2.2 %shard_map.111 = (f32[1,256]{1,0:T(1,128)}, f32[1,256]{1,0:T(1,128)}, bf16[768,512]{1,0:T(8,128)(2,1)S(1)}, bf16[768,512]{1,0:T(8,128)(2,1)S(1)}) custom-call(s32[8]{0:T(128)S(1)} %get-tuple-element.30.slots_ref, bf16[4,256,256]{2,1,0:T(8,128)(2,1)S(1)} %get-tuple-element.31.phi_hi, ...), custom_call_target="tpu_custom_call", output_to_operand_aliasing={{2}: (8, {}), {3}: (9, {})} | custom-call | bytes 2097152 | tf_op jit(solution)/shard_map/pallas_call | solution.py:352
Async XLA Ops:
  0.6 10.7 %collective-permute-start = (f32[256,128]{1,0:T(8,128)}, f32[256,128]{1,0:T(8,128)S(1)}, u32[]{:S(2)}, u32[]{:S(2)}) collective-permute-start(f32[256,128]{1,0:T(8,128)} %refs_3_.2), channel_id=1, source_target_pairs={{0,2},{1,3},{2,0},{3,1},{4,6},{5,7},{6,4},{7,5},{8,10},{9,11},{10,... | collective-permute-start | bytes 393224 | tf_op jit(solution)/shard_map/ppermute | solution.py:35
  4.8 9.3 %collective-permute-start.4 = (f32[96,512]{1,0:T(8,128)}, f32[96,512]{1,0:T(8,128)S(1)}, u32[]{:S(2)}, u32[]{:S(2)}) collective-permute-start(f32[96,512]{1,0:T(8,128)} %refs_4_.2), channel_id=1, source_target_pairs={{0,8},{4,12},{8,0},{12,4},{16,24},{20,28},{24,16},{28,20},{1,9},{5... | collective-permute-start | bytes 589832 | tf_op jit(solution)/shard_map/ppermute | solution.py:35
  6.3 10.5 %collective-permute-start.5 = (f32[96,512]{1,0:T(8,128)}, f32[96,512]{1,0:T(8,128)S(1)}, u32[]{:S(2)}, u32[]{:S(2)}) collective-permute-start(f32[96,512]{1,0:T(8,128)} %refs_4_.2), channel_id=1, source_target_pairs={{0,16},{4,20},{8,24},{12,28},{16,0},{20,4},{24,8},{28,12},{1,17},{... | collective-permute-start | bytes 589832 | tf_op jit(solution)/shard_map/ppermute | solution.py:35
  7.8 9.0 %collective-permute-start.6 = (f32[96,512]{1,0:T(8,128)}, f32[96,512]{1,0:T(8,128)S(1)}, u32[]{:S(2)}, u32[]{:S(2)}) collective-permute-start(f32[96,512]{1,0:T(8,128)} %refs_4_.2), channel_id=1, source_target_pairs={{0,24},{4,28},{8,16},{12,20},{16,8},{20,12},{24,0},{28,4},{1,25},{... | collective-permute-start | bytes 589832 | tf_op jit(solution)/shard_map/ppermute | solution.py:35
  8.2 5.8 %collective-permute-start.2 = (f32[256,128]{1,0:T(8,128)}, f32[256,128]{1,0:T(8,128)S(1)}, u32[]{:S(2)}, u32[]{:S(2)}) collective-permute-start(f32[256,128]{1,0:T(8,128)} %refs_3_.2), channel_id=1, source_target_pairs={{0,1},{1,0},{2,3},{3,2},{4,5},{5,4},{6,7},{7,6},{8,9},{9,8},{10,11... | collective-permute-start | bytes 393224 | tf_op jit(solution)/shard_map/ppermute | solution.py:35
  11.4 11.3 %collective-permute-start.12 = (f32[96,512]{1,0:T(8,128)}, f32[96,512]{1,0:T(8,128)S(1)}, u32[]{:S(2)}, u32[]{:S(2)}) collective-permute-start(f32[96,512]{1,0:T(8,128)} %refs_4_.2), channel_id=1, source_target_pairs={{0,2},{1,3},{2,0},{3,1},{4,6},{5,7},{6,4},{7,5},{8,10},{9,11},{10,... | collective-permute-start | bytes 589832 | tf_op jit(solution)/shard_map/ppermute | solution.py:35
  14.1 9.9 %collective-permute-start.3 = (f32[96,512]{1,0:T(8,128)}, f32[96,512]{1,0:T(8,128)S(1)}, u32[]{:S(2)}, u32[]{:S(2)}) collective-permute-start(f32[96,512]{1,0:T(8,128)} %refs_4_.2), channel_id=1, source_target_pairs={{0,4},{4,0},{8,12},{12,8},{16,20},{20,16},{24,28},{28,24},{1,5},{5... | collective-permute-start | bytes 589832 | tf_op jit(solution)/shard_map/ppermute | solution.py:35
  14.1 9.9 %collective-permute-start.7 = (f32[96,512]{1,0:T(8,128)S(1)}, f32[96,512]{1,0:T(8,128)S(1)}, u32[]{:S(2)}, u32[]{:S(2)}) collective-permute-start(f32[96,512]{1,0:T(8,128)S(1)} %collective-permute-done.4.refs_4_), channel_id=1, source_target_pairs={{0,4},{4,0},{8,12},{12,8},{16,20},{20,16},{24,28},{28,24},{1,5},{5... | collective-permute-start | bytes 589832 | tf_op jit(solution)/shard_map/ppermute | solution.py:35
  16.8 8.8 %collective-permute-start.8 = (f32[96,512]{1,0:T(8,128)S(1)}, f32[96,512]{1,0:T(8,128)S(1)}, u32[]{:S(2)}, u32[]{:S(2)}) collective-permute-start(f32[96,512]{1,0:T(8,128)S(1)} %collective-permute-done.5.refs_5_), channel_id=1, source_target_pairs={{0,4},{4,0},{8,12},{12,8},{16,20},{20,16},{24,28},{28,24},{1,5},{5... | collective-permute-start | bytes 589832 | tf_op jit(solution)/shard_map/ppermute | solution.py:35
  16.8 9.5 %collective-permute-start.9 = (f32[96,512]{1,0:T(8,128)S(1)}, f32[96,512]{1,0:T(8,128)S(1)}, u32[]{:S(2)}, u32[]{:S(2)}) collective-permute-start(f32[96,512]{1,0:T(8,128)S(1)} %collective-permute-done.6.refs_6_), channel_id=1, source_target_pairs={{0,4},{4,0},{8,12},{12,8},{16,20},{20,16},{24,28},{28,24},{1,5},{5... | collective-permute-start | bytes 589832 | tf_op jit(solution)/shard_map/ppermute | solution.py:35
  22.7 10.3 %collective-permute-start.14 = (f32[96,512]{1,0:T(8,128)S(1)}, f32[96,512]{1,0:T(8,128)S(1)}, u32[]{:S(2)}, u32[]{:S(2)}) collective-permute-start(f32[96,512]{1,0:T(8,128)S(1)} %collective-permute-done.12.refs_2_), channel_id=1, source_target_pairs={{0,8},{4,12},{8,0},{12,4},{16,24},{20,28},{24,16},{28,20},{1,9},{5... | collective-permute-start | bytes 589832 | tf_op jit(solution)/shard_map/ppermute | solution.py:35
  24.0 5.8 %collective-permute-start.1 = (f32[256,128]{1,0:T(8,128)S(1)}, f32[256,128]{1,0:T(8,128)S(1)}, u32[]{:S(2)}, u32[]{:S(2)}) collective-permute-start(f32[256,128]{1,0:T(8,128)S(1)} %collective-permute-done.refs_1_), channel_id=1, source_target_pairs={{0,1},{1,0},{2,3},{3,2},{4,5},{5,4},{6,7},{7,6},{8,9},{9,8},{10,11... | collective-permute-start | bytes 393224 | tf_op jit(solution)/shard_map/ppermute | solution.py:35
  24.0 10.3 %collective-permute-start.15 = (f32[96,512]{1,0:T(8,128)S(1)}, f32[96,512]{1,0:T(8,128)S(1)}, u32[]{:S(2)}, u32[]{:S(2)}) collective-permute-start(f32[96,512]{1,0:T(8,128)S(1)} %collective-permute-done.12.refs_2_), channel_id=1, source_target_pairs={{0,16},{4,20},{8,24},{12,28},{16,0},{20,4},{24,8},{28,12},{1,17},{... | collective-permute-start | bytes 589832 | tf_op jit(solution)/shard_map/ppermute | solution.py:35
  25.6 8.7 %collective-permute-start.16 = (f32[96,512]{1,0:T(8,128)S(1)}, f32[96,512]{1,0:T(8,128)S(1)}, u32[]{:S(2)}, u32[]{:S(2)}) collective-permute-start(f32[96,512]{1,0:T(8,128)S(1)} %collective-permute-done.12.refs_2_), channel_id=1, source_target_pairs={{0,24},{4,28},{8,16},{12,20},{16,8},{20,12},{24,0},{28,4},{1,25},{... | collective-permute-start | bytes 589832 | tf_op jit(solution)/shard_map/ppermute | solution.py:35
  26.2 8.6 %collective-permute-start.13 = (f32[96,512]{1,0:T(8,128)S(1)}, f32[96,512]{1,0:T(8,128)S(1)}, u32[]{:S(2)}, u32[]{:S(2)}) collective-permute-start(f32[96,512]{1,0:T(8,128)S(1)} %collective-permute-done.12.refs_2_), channel_id=1, source_target_pairs={{0,4},{4,0},{8,12},{12,8},{16,20},{20,16},{24,28},{28,24},{1,5},{5... | collective-permute-start | bytes 589832 | tf_op jit(solution)/shard_map/ppermute | solution.py:35
  30.3 11.1 %collective-permute-start.10 = (f32[256,256]{1,0:T(8,128)S(1)}, f32[256,256]{1,0:T(8,128)S(1)}, u32[]{:S(2)}, u32[]{:S(2)}) collective-permute-start(f32[256,256]{1,0:T(8,128)S(1)} %get-tuple-element.49), channel_id=1, source_target_pairs={{0,3},{1,2},{2,1},{3,0},{4,7},{5,6},{6,5},{7,4},{8,11},{9,10},{10,... | collective-permute-start | bytes 786440 | tf_op jit(solution)/shard_map/ppermute | solution.py:35
  33.0 13.7 %collective-permute-start.11 = (f32[256,256]{1,0:T(8,128)S(1)}, f32[256,256]{1,0:T(8,128)S(1)}, u32[]{:S(2)}, u32[]{:S(2)}) collective-permute-start(f32[256,256]{1,0:T(8,128)S(1)} %get-tuple-element.50), channel_id=1, source_target_pairs={{0,1},{1,0},{2,3},{3,2},{4,5},{5,4},{6,7},{7,6},{8,9},{9,8},{10,11... | collective-permute-start | bytes 786440 | tf_op jit(solution)/shard_map/ppermute | solution.py:35
  34.3 12.9 %collective-permute-start.17 = (f32[96,512]{1,0:T(8,128)S(1)}, f32[96,512]{1,0:T(8,128)S(1)}, u32[]{:S(2)}, u32[]{:S(2)}) collective-permute-start(f32[96,512]{1,0:T(8,128)S(1)} %collective-permute-done.14.refs_4_), channel_id=1, source_target_pairs={{0,4},{4,0},{8,12},{12,8},{16,20},{20,16},{24,28},{28,24},{1,5},{5... | collective-permute-start | bytes 589832 | tf_op jit(solution)/shard_map/ppermute | solution.py:35
  34.3 12.9 %collective-permute-start.18 = (f32[96,512]{1,0:T(8,128)S(1)}, f32[96,512]{1,0:T(8,128)S(1)}, u32[]{:S(2)}, u32[]{:S(2)}) collective-permute-start(f32[96,512]{1,0:T(8,128)S(1)} %collective-permute-done.15.refs_5_), channel_id=1, source_target_pairs={{0,4},{4,0},{8,12},{12,8},{16,20},{20,16},{24,28},{28,24},{1,5},{5... | collective-permute-start | bytes 589832 | tf_op jit(solution)/shard_map/ppermute | solution.py:35
  34.8 12.4 %collective-permute-start.19 = (f32[96,512]{1,0:T(8,128)S(1)}, f32[96,512]{1,0:T(8,128)S(1)}, u32[]{:S(2)}, u32[]{:S(2)}) collective-permute-start(f32[96,512]{1,0:T(8,128)S(1)} %collective-permute-done.16.refs_6_), channel_id=1, source_target_pairs={{0,4},{4,0},{8,12},{12,8},{16,20},{20,16},{24,28},{28,24},{1,5},{5... | collective-permute-start | bytes 589832 | tf_op jit(solution)/shard_map/ppermute | solution.py:35
